TPU v7x, 512 devices: a whole 4x4x16 slice. The times are simulated.
512 devices in a mesh: tm: 128 (over z, y, core), col: 4 (over x).
Axes of the slice: x: 4, y: 4, z: 16, core: 2. Of those that a mesh axis runs over, the one named last changes fastest.
Arguments:
- gain: float32 [128, 256, 256], P('tm', None, 'col')
- offset: float32 [128, 256], P('tm'), may hold values from -4 to 4
- sub_offset: float32 [128, 8, 256], P('tm'), may hold values from -6 to 6
- terminal_state: float32 [256], replicated, may hold values from -6 to 6
- terminal_factor: float32 [256, 256], replicated, may hold values from -0.375 to 0.375
- obs_rows: bfloat16 [131072, 256], P('tm', 'col'), may hold values from -0.375 to 0.375
- obs_count: int32 [128], P('tm'), may hold values from 256 to 1024, as said below
- obs_step: int32 [131072], P('tm'), may hold values from 0 to 7
Outputs:
- predicted: float32 [131072], P('tm')
- leverage: float32 [131072], P('tm')
Inputs may be any that keep to these rules, and one draw needn't show every extreme that they name: `obs_count`: each group has at least a quarter of its slots live; some group has all 1024 live.
All inputs are finite; a program needn't handle non-finite values.
Results may differ from a plain program's by a relative error of at most 0.0029.
Values may be sent and summed in bfloat16 or wider, within the bound.
No kernel may reach another device: no remote copies, remote signals or barrier semaphores. Data moves between devices by JAX's collectives and lax.ppermute only.
A program may use at most 64 MiB of HBM per device.

v0:
```python
import jax
import jax.numpy as jnp
from jax import lax
from jax.sharding import PartitionSpec as P

S = 256
SUB = 8


def passed_along(shard, axis, by):
    peers = lax.axis_size(axis)
    pairs = [(i, i + by) for i in range(peers) if 0 <= i + by < peers]
    return lax.ppermute(shard, axis, pairs)


def shards(
    gain, offset, sub_offset, terminal_state, terminal_factor, obs_rows, obs_count, obs_step
):
    highest = lax.Precision.HIGHEST
    block = lax.all_gather(gain[0], "col", axis=1, tiled=True)
    bias = offset[0]
    width = S // lax.axis_size("col")
    first_col = lax.axis_index("col") * width
    group_count = lax.axis_size("tm")
    group_index = lax.axis_index("tm")
    eye_map = jnp.eye(S, dtype=jnp.float32)
    zero_vec = jnp.zeros((S,), jnp.float32)
    next_map, next_vec = passed_along((block, bias), "tm", -1)
    has_next = group_index + 1 < group_count
    composed = jnp.where(has_next, next_map, eye_map)
    shifted = jnp.where(has_next, next_vec, zero_vec)
    distance = 1
    while distance < group_count:
        far_map, far_vec = passed_along((composed, shifted), "tm", -distance)
        reach = group_index + distance < group_count
        far_map = jnp.where(reach, far_map, eye_map)
        far_vec = jnp.where(reach, far_vec, zero_vec)
        shifted = jnp.dot(composed, far_vec, precision=highest) + shifted
        composed = jnp.dot(composed, far_map, precision=highest)
        distance = distance * 2
    upcoming = jnp.dot(composed, terminal_state, precision=highest) + shifted
    state = jnp.dot(block, upcoming, precision=highest) + bias
    full_map = jnp.dot(block, composed, precision=highest)
    states = (state[None, :] + sub_offset[0]).astype(jnp.bfloat16)
    state_cols = lax.dynamic_slice_in_dim(states, first_col, width, 1)
    picks = jnp.dot(obs_rows, state_cols.T, preferred_element_type=jnp.float32)
    step_ids = jnp.arange(SUB)
    onehot = obs_step[:, None] == step_ids[None, :]
    guess_part = jnp.sum(jnp.where(onehot, picks, jnp.float32(0.0)), axis=1)
    map_rows = lax.dynamic_slice_in_dim(full_map, first_col, width, 0)
    factor_rows = jnp.dot(
        map_rows, terminal_factor, precision=highest, preferred_element_type=jnp.float32
    ).astype(jnp.bfloat16)
    projected = lax.psum_scatter(
        lax.dot_general(
            factor_rows, obs_rows, (((0,), (1,)), ((), ())), preferred_element_type=jnp.float32
        ),
        "col",
        scatter_dimension=0,
        tiled=True,
    )
    spread_part = jnp.sum(projected * projected, axis=0)
    guess, spread = lax.psum((guess_part, spread_part), "col")
    slot_ids = jnp.arange(obs_rows.shape[0])
    live = (slot_ids < obs_count[0]).astype(jnp.float32)
    return (guess * live, spread * live)


def solution(mesh):
    in_specs = (
        P("tm", None, "col"),
        P("tm", None),
        P("tm", None, None),
        P(),
        P(),
        P("tm", "col"),
        P("tm"),
        P("tm"),
    )
    out_specs = (P("tm"), P("tm"))
    return jax.shard_map(shards, mesh=mesh, in_specs=in_specs, out_specs=out_specs, check_vma=False)
```

profile of v0, /device:TPU:48, one launch (start us, length us, event | category | flops | bytes accessed | tf_op | source)
XLA Modules:
  0.0 200.2 jit_solution(14800867112402248286)
XLA Ops:
  7.2 0.9 copy.11
  8.2 12.6 %all-gather = f32[1,256,256]{1,0,2:T(1,128)S(1)} all-gather(f32[1,256,64]{1,0,2:T(1,128)S(1)} %copy.11), channel_id=2, replica_groups=mesh['tm'=128,'col'=4] {'col'}, dimensions={2}, use_global_device_ids=true | all-gather | bytes 327680 | tf_op jit(solution)/shard_map/all_gather | solution.py:20
  20.9 1.9 collective-permute-start
  22.9 3.9 %collective-permute-done = f32[256,256]{1,0:T(8,128)S(1)} collective-permute-done((f32[256,256]{1,0:T(8,128)S(1)}, f32[256,256]{1,0:T(8,128)S(1)}, u32[]{:S(2)}, u32[]{:S(2)}) %collective-permute-start) | collective-permute-done | bytes 262176 | tf_op jit(solution)/shard_map/ppermute | solution.py:13
  26.7 3.8 %collective-permute-start.1 = (f32[256,256]{1,0:T(8,128)S(1)}, f32[256,256]{1,0:T(8,128)S(1)}, u32[]{:S(2)}, u32[]{:S(2)}) collective-permute-start(f32[256,256]{1,0:T(8,128)S(1)} %convert_select_fusion.7), channel_id=1, source_target_pairs={{4,0},{8,4},{12,8},{16,12},{20,16},{24,20},{28,24},{32,28},{36,32}... | collective-permute-start | bytes 786440 | tf_op jit(solution)/shard_map/ppermute | solution.py:13
  30.6 3.9 %collective-permute-done.1 = f32[256,256]{1,0:T(8,128)S(1)} collective-permute-done((f32[256,256]{1,0:T(8,128)S(1)}, f32[256,256]{1,0:T(8,128)S(1)}, u32[]{:S(2)}, u32[]{:S(2)}) %collective-permute-start.1) | collective-permute-done | bytes 262176 | tf_op jit(solution)/shard_map/ppermute | solution.py:13
  34.4 0.4 fusion.2
  34.9 2.4 %collective-permute-start.2 = (f32[256,256]{1,0:T(8,128)S(1)}, f32[256,256]{1,0:T(8,128)S(1)}, u32[]{:S(2)}, u32[]{:S(2)}) collective-permute-start(f32[256,256]{1,0:T(8,128)S(1)} %fusion.2), channel_id=1, source_target_pairs={{8,0},{12,4},{16,8},{20,12},{24,16},{28,20},{32,24},{36,28},{40,32... | collective-permute-start | bytes 786440 | tf_op jit(solution)/shard_map/ppermute | solution.py:13
  37.2 3.5 %collective-permute-start.8 = (f32[256]{0:T(256)S(1)}, f32[256]{0:T(256)S(1)}, u32[]{:S(2)}, u32[]{:S(2)}) collective-permute-start(f32[256]{0:T(256)S(1)} %bitcast.82), channel_id=1, source_target_pairs={{4,0},{8,4},{12,8},{16,12},{20,16},{24,20},{28,24},{32,28},{36,32}... | collective-permute-start | bytes 3080 | tf_op jit(solution)/shard_map/ppermute | solution.py:13
  40.8 2.6 %collective-permute-done.2 = f32[256,256]{1,0:T(8,128)S(1)} collective-permute-done((f32[256,256]{1,0:T(8,128)S(1)}, f32[256,256]{1,0:T(8,128)S(1)}, u32[]{:S(2)}, u32[]{:S(2)}) %collective-permute-start.2) | collective-permute-done | bytes 262176 | tf_op jit(solution)/shard_map/ppermute | solution.py:13
  43.4 0.4 fusion.3
  43.8 5.7 %collective-permute-start.3 = (f32[256,256]{1,0:T(8,128)S(1)}, f32[256,256]{1,0:T(8,128)S(1)}, u32[]{:S(2)}, u32[]{:S(2)}) collective-permute-start(f32[256,256]{1,0:T(8,128)S(1)} %fusion.3), channel_id=1, source_target_pairs={{16,0},{20,4},{24,8},{28,12},{32,16},{36,20},{40,24},{44,28},{48,3... | collective-permute-start | bytes 786440 | tf_op jit(solution)/shard_map/ppermute | solution.py:13
  49.5 4.4 %collective-permute-start.9 = (f32[256]{0:T(256)S(1)}, f32[256]{0:T(256)S(1)}, u32[]{:S(2)}, u32[]{:S(2)}) collective-permute-start(f32[256]{0:T(256)S(1)} %broadcast_select_fusion.1), channel_id=1, source_target_pairs={{4,0},{8,4},{12,8},{16,12},{20,16},{24,20},{28,24},{32,28},{36,32}... | collective-permute-start | bytes 3080 | tf_op jit(solution)/shard_map/ppermute | solution.py:13
  54.0 1.3 collective-permute-done.9
  55.2 2.0 %collective-permute-done.3 = f32[256,256]{1,0:T(8,128)S(1)} collective-permute-done((f32[256,256]{1,0:T(8,128)S(1)}, f32[256,256]{1,0:T(8,128)S(1)}, u32[]{:S(2)}, u32[]{:S(2)}) %collective-permute-start.3) | collective-permute-done | bytes 262176 | tf_op jit(solution)/shard_map/ppermute | solution.py:13
  57.3 0.4 fusion.4
  57.7 3.4 %collective-permute-start.4 = (f32[256,256]{1,0:T(8,128)S(1)}, f32[256,256]{1,0:T(8,128)S(1)}, u32[]{:S(2)}, u32[]{:S(2)}) collective-permute-start(f32[256,256]{1,0:T(8,128)S(1)} %fusion.4), channel_id=1, source_target_pairs={{32,0},{36,4},{40,8},{44,12},{48,16},{52,20},{56,24},{60,28},{64,3... | collective-permute-start | bytes 786440 | tf_op jit(solution)/shard_map/ppermute | solution.py:13
  61.1 0.3 fusion.29
  61.4 2.8 %collective-permute-start.10 = (f32[256]{0:T(256)S(1)}, f32[256]{0:T(256)S(1)}, u32[]{:S(2)}, u32[]{:S(2)}) collective-permute-start(f32[256]{0:T(256)S(1)} %fusion.66), channel_id=1, source_target_pairs={{8,0},{12,4},{16,8},{20,12},{24,16},{28,20},{32,24},{36,28},{40,32... | collective-permute-start | bytes 3080 | tf_op jit(solution)/shard_map/ppermute | solution.py:13
  64.3 4.2 %collective-permute-done.4 = f32[256,256]{1,0:T(8,128)S(1)} collective-permute-done((f32[256,256]{1,0:T(8,128)S(1)}, f32[256,256]{1,0:T(8,128)S(1)}, u32[]{:S(2)}, u32[]{:S(2)}) %collective-permute-start.4) | collective-permute-done | bytes 262176 | tf_op jit(solution)/shard_map/ppermute | solution.py:13
  68.5 0.4 fusion.5
  68.9 1.3 collective-permute-start.5
  70.2 0.3 fusion.30
  70.5 2.0 collective-permute-start.11
  72.5 15.7 %collective-permute-done.5 = f32[256,256]{1,0:T(8,128)S(1)} collective-permute-done((f32[256,256]{1,0:T(8,128)S(1)}, f32[256,256]{1,0:T(8,128)S(1)}, u32[]{:S(2)}, u32[]{:S(2)}) %collective-permute-start.5) | collective-permute-done | bytes 262176 | tf_op jit(solution)/shard_map/ppermute | solution.py:13
  88.2 0.4 fusion.6
  88.6 1.3 collective-permute-start.6
  90.2 2.0 collective-permute-start.12
  92.2 25.1 %collective-permute-done.6 = f32[256,256]{1,0:T(8,128)S(1)} collective-permute-done((f32[256,256]{1,0:T(8,128)S(1)}, f32[256,256]{1,0:T(8,128)S(1)}, u32[]{:S(2)}, u32[]{:S(2)}) %collective-permute-start.6) | collective-permute-done | bytes 262176 | tf_op jit(solution)/shard_map/ppermute | solution.py:13
  117.3 0.4 fusion.7
  117.7 1.3 collective-permute-start.7
  119.3 1.3 collective-permute-start.13
  120.6 31.2 %collective-permute-done.7 = f32[256,256]{1,0:T(8,128)S(1)} collective-permute-done((f32[256,256]{1,0:T(8,128)S(1)}, f32[256,256]{1,0:T(8,128)S(1)}, u32[]{:S(2)}, u32[]{:S(2)}) %collective-permute-start.7) | collective-permute-done | bytes 262176 | tf_op jit(solution)/shard_map/ppermute | solution.py:13
  151.8 0.4 fusion.8
  152.2 0.6 fusion.24
  152.9 0.5 convolution_convert_fusion
  153.3 0.4 copy-done.1
  153.8 1.3 fusion.36
  155.4 1.3 collective-permute-start.14
  156.7 8.1 %collective-permute-done.14 = f32[256]{0:T(256)S(1)} collective-permute-done((f32[256]{0:T(256)S(1)}, f32[256]{0:T(256)S(1)}, u32[]{:S(2)}, u32[]{:S(2)}) %collective-permute-start.14) | collective-permute-done | bytes 1056 | tf_op jit(solution)/shard_map/ppermute | solution.py:13
  165.1 1.3 collective-permute-start.15
  167.1 12.2 %collective-permute-done.15 = f32[256]{0:T(256)S(1)} collective-permute-done((f32[256]{0:T(256)S(1)}, f32[256]{0:T(256)S(1)}, u32[]{:S(2)}, u32[]{:S(2)}) %collective-permute-start.15) | collective-permute-done | bytes 1056 | tf_op jit(solution)/shard_map/ppermute | solution.py:13
  179.6 0.7 copy-done.4
  181.1 0.3 copy-done.3
  181.4 0.3 copy-done.2
  181.9 1.0 multiply_reduce_fusion
  182.9 9.8 %all-reduce = (f32[1024]{0:T(1024)S(1)}, f32[1024]{0:T(1024)S(1)}) all-reduce(f32[1024]{0:T(1024)S(1)} %fusion.1, f32[1024]{0:T(1024)S(1)} %multiply_reduce_fusion), channel_id=1, replica_groups=mesh['tm'=128,'col'=4] {'col'}, use_global_device_ids=true, to_apply=%region_1.2 | all-reduce | flops 2048 | bytes 16384 | tf_op jit(solution)/shard_map/psum | solution.py:63
  192.8 0.6 fusion.18
  (43 shorter events, 2.6 us)
Async XLA Ops:
  7.2 145.7 %copy-start = (f32[256,256]{1,0:T(8,128)S(1)}, f32[256,256]{1,0:T(8,128)}, u32[]{:S(2)}) copy-start(f32[256,256]{1,0:T(8,128)} %param.12) | copy-start | bytes 786436
  7.2 174.7 %reduce-scatter.2.cloned.1.call-start = ((), (), s32[]{:S(2)}) async-start(), calls=%async_computation.1 | async-start | bytes 1310720 | tf_op jit(solution)/shard_map/reduce_scatter | solution.py:54
  20.9 5.8 %collective-permute-start = (f32[256,256]{1,0:T(8,128)S(1)}, f32[256,256]{1,0:T(8,128)S(1)}, u32[]{:S(2)}, u32[]{:S(2)}) collective-permute-start(f32[256,256]{1,0:T(8,128)S(1)} %bitcast.62), channel_id=1, source_target_pairs={{4,0},{8,4},{12,8},{16,12},{20,16},{24,20},{28,24},{32,28},{36,32}... | collective-permute-start | bytes 786440 | tf_op jit(solution)/shard_map/ppermute | solution.py:13
  26.7 7.7 %collective-permute-start.1 = (f32[256,256]{1,0:T(8,128)S(1)}, f32[256,256]{1,0:T(8,128)S(1)}, u32[]{:S(2)}, u32[]{:S(2)}) collective-permute-start(f32[256,256]{1,0:T(8,128)S(1)} %convert_select_fusion.7), channel_id=1, source_target_pairs={{4,0},{8,4},{12,8},{16,12},{20,16},{24,20},{28,24},{32,28},{36,32}... | collective-permute-start | bytes 786440 | tf_op jit(solution)/shard_map/ppermute | solution.py:13
  34.8 2.4 %copy-start.5 = (f32[1,256]{1,0:T(1,128)S(1)}, f32[1,256]{1,0:T(1,128)}, u32[]{:S(2)}) copy-start(f32[1,256]{1,0:T(1,128)} %param.9) | copy-start | bytes 3076
  34.9 8.5 %collective-permute-start.2 = (f32[256,256]{1,0:T(8,128)S(1)}, f32[256,256]{1,0:T(8,128)S(1)}, u32[]{:S(2)}, u32[]{:S(2)}) collective-permute-start(f32[256,256]{1,0:T(8,128)S(1)} %fusion.2), channel_id=1, source_target_pairs={{8,0},{12,4},{16,8},{20,12},{24,16},{28,20},{32,24},{36,28},{40,32... | collective-permute-start | bytes 786440 | tf_op jit(solution)/shard_map/ppermute | solution.py:13
  37.2 12.2 %collective-permute-start.8 = (f32[256]{0:T(256)S(1)}, f32[256]{0:T(256)S(1)}, u32[]{:S(2)}, u32[]{:S(2)}) collective-permute-start(f32[256]{0:T(256)S(1)} %bitcast.82), channel_id=1, source_target_pairs={{4,0},{8,4},{12,8},{16,12},{20,16},{24,20},{28,24},{32,28},{36,32}... | collective-permute-start | bytes 3080 | tf_op jit(solution)/shard_map/ppermute | solution.py:13
  43.8 13.5 %collective-permute-start.3 = (f32[256,256]{1,0:T(8,128)S(1)}, f32[256,256]{1,0:T(8,128)S(1)}, u32[]{:S(2)}, u32[]{:S(2)}) collective-permute-start(f32[256,256]{1,0:T(8,128)S(1)} %fusion.3), channel_id=1, source_target_pairs={{16,0},{20,4},{24,8},{28,12},{32,16},{36,20},{40,24},{44,28},{48,3... | collective-permute-start | bytes 786440 | tf_op jit(solution)/shard_map/ppermute | solution.py:13
  49.5 5.7 %collective-permute-start.9 = (f32[256]{0:T(256)S(1)}, f32[256]{0:T(256)S(1)}, u32[]{:S(2)}, u32[]{:S(2)}) collective-permute-start(f32[256]{0:T(256)S(1)} %broadcast_select_fusion.1), channel_id=1, source_target_pairs={{4,0},{8,4},{12,8},{16,12},{20,16},{24,20},{28,24},{32,28},{36,32}... | collective-permute-start | bytes 3080 | tf_op jit(solution)/shard_map/ppermute | solution.py:13
  57.7 10.8 %collective-permute-start.4 = (f32[256,256]{1,0:T(8,128)S(1)}, f32[256,256]{1,0:T(8,128)S(1)}, u32[]{:S(2)}, u32[]{:S(2)}) collective-permute-start(f32[256,256]{1,0:T(8,128)S(1)} %fusion.4), channel_id=1, source_target_pairs={{32,0},{36,4},{40,8},{44,12},{48,16},{52,20},{56,24},{60,28},{64,3... | collective-permute-start | bytes 786440 | tf_op jit(solution)/shard_map/ppermute | solution.py:13
  61.4 8.8 %collective-permute-start.10 = (f32[256]{0:T(256)S(1)}, f32[256]{0:T(256)S(1)}, u32[]{:S(2)}, u32[]{:S(2)}) collective-permute-start(f32[256]{0:T(256)S(1)} %fusion.66), channel_id=1, source_target_pairs={{8,0},{12,4},{16,8},{20,12},{24,16},{28,20},{32,24},{36,28},{40,32... | collective-permute-start | bytes 3080 | tf_op jit(solution)/shard_map/ppermute | solution.py:13
  68.9 19.3 %collective-permute-start.5 = (f32[256,256]{1,0:T(8,128)S(1)}, f32[256,256]{1,0:T(8,128)S(1)}, u32[]{:S(2)}, u32[]{:S(2)}) collective-permute-start(f32[256,256]{1,0:T(8,128)S(1)} %fusion.5), channel_id=1, source_target_pairs={{64,0},{68,4},{72,8},{76,12},{80,16},{84,20},{88,24},{92,28},{96,3... | collective-permute-start | bytes 786440 | tf_op jit(solution)/shard_map/ppermute | solution.py:13
  70.5 19.4 %collective-permute-start.11 = (f32[256]{0:T(256)S(1)}, f32[256]{0:T(256)S(1)}, u32[]{:S(2)}, u32[]{:S(2)}) collective-permute-start(f32[256]{0:T(256)S(1)} %add.75), channel_id=1, source_target_pairs={{16,0},{20,4},{24,8},{28,12},{32,16},{36,20},{40,24},{44,28},{48,3... | collective-permute-start | bytes 3080 | tf_op jit(solution)/shard_map/ppermute | solution.py:13
  88.6 28.7 %collective-permute-start.6 = (f32[256,256]{1,0:T(8,128)S(1)}, f32[256,256]{1,0:T(8,128)S(1)}, u32[]{:S(2)}, u32[]{:S(2)}) collective-permute-start(f32[256,256]{1,0:T(8,128)S(1)} %fusion.6), channel_id=1, source_target_pairs={{128,0},{132,4},{136,8},{140,12},{144,16},{148,20},{152,24},{156,2... | collective-permute-start | bytes 786440 | tf_op jit(solution)/shard_map/ppermute | solution.py:13
  90.2 28.8 %collective-permute-start.12 = (f32[256]{0:T(256)S(1)}, f32[256]{0:T(256)S(1)}, u32[]{:S(2)}, u32[]{:S(2)}) collective-permute-start(f32[256]{0:T(256)S(1)} %add.76), channel_id=1, source_target_pairs={{32,0},{36,4},{40,8},{44,12},{48,16},{52,20},{56,24},{60,28},{64,3... | collective-permute-start | bytes 3080 | tf_op jit(solution)/shard_map/ppermute | solution.py:13
  117.7 34.1 %collective-permute-start.7 = (f32[256,256]{1,0:T(8,128)S(1)}, f32[256,256]{1,0:T(8,128)S(1)}, u32[]{:S(2)}, u32[]{:S(2)}) collective-permute-start(f32[256,256]{1,0:T(8,128)S(1)} %fusion.7), channel_id=1, source_target_pairs={{256,0},{260,4},{264,8},{268,12},{272,16},{276,20},{280,24},{284,2... | collective-permute-start | bytes 786440 | tf_op jit(solution)/shard_map/ppermute | solution.py:13
  119.3 35.8 %collective-permute-start.13 = (f32[256]{0:T(256)S(1)}, f32[256]{0:T(256)S(1)}, u32[]{:S(2)}, u32[]{:S(2)}) collective-permute-start(f32[256]{0:T(256)S(1)} %add.77), channel_id=1, source_target_pairs={{64,0},{68,4},{72,8},{76,12},{80,16},{84,20},{88,24},{92,28},{96,3... | collective-permute-start | bytes 3080 | tf_op jit(solution)/shard_map/ppermute | solution.py:13
  152.9 0.9 copy-start.1
  155.4 9.4 %collective-permute-start.14 = (f32[256]{0:T(256)S(1)}, f32[256]{0:T(256)S(1)}, u32[]{:S(2)}, u32[]{:S(2)}) collective-permute-start(f32[256]{0:T(256)S(1)} %add.78), channel_id=1, source_target_pairs={{128,0},{132,4},{136,8},{140,12},{144,16},{148,20},{152,24},{156,2... | collective-permute-start | bytes 3080 | tf_op jit(solution)/shard_map/ppermute | solution.py:13
  165.1 14.2 %collective-permute-start.15 = (f32[256]{0:T(256)S(1)}, f32[256]{0:T(256)S(1)}, u32[]{:S(2)}, u32[]{:S(2)}) collective-permute-start(f32[256]{0:T(256)S(1)} %add.79), channel_id=1, source_target_pairs={{256,0},{260,4},{264,8},{268,12},{272,16},{276,20},{280,24},{284,2... | collective-permute-start | bytes 3080 | tf_op jit(solution)/shard_map/ppermute | solution.py:13
  179.6 0.7 copy-start.4
  180.6 0.8 copy-start.3
  180.9 0.8 copy-start.2
Sparse Core Ops, SparseCore 0:
  155.2 24.3 reduce-scatter.1
where the time goes:
time: 201 us; the launch traced here: 200 us
  waiting for transfers between devices  110 us (55%)
  starting transfers between devices  39.9 us (20%)
  blocking collectives  22.5 us (11%)
  between operations  15.1 us (8%)
  matrix products  7.76 us (4%)
  local copies, waits for them, and re-layouts  3.01 us (1%)
    ppermute x16, waiting for transfers between devices, passed_along(): return lax.ppermute(shard, axis, pairs)  110 us
    ppermute x16, starting transfers between devices, passed_along(): return lax.ppermute(shard, axis, pairs)  39.8 us
    all_gather x1, blocking collectives, shards(): block = lax.all_gather(gain[0], 'col', axis=1, tiled=True)  12.6 us
    psum x1, blocking collectives, shards(): guess, spread = lax.psum((guess_part, spread_part), 'col')  9.85 us
  transfers between devices with their start and end apart: 17, of which 11 were waited for; matrix products, arithmetic and copies ran while one was open for 4% of the time, Pallas kernels for 0%

commit v1 on v0

v1 whole, which is shorter than its diff:
```python
import jax
import jax.numpy as jnp
from jax import lax
from jax.sharding import Mesh, PartitionSpec as P

S = 256
SUB = 8
AUG = 264
NZ, NY, NC, NX = 16, 4, 2, 4
TM = ("z", "y", "core")
HIGHEST = lax.Precision.HIGHEST


def tm_id(z, y, c):
    return (z * NY + y) * NC + c


def bias_rows(vec, rows):
    return jnp.zeros((rows, S), jnp.float32).at[rows - SUB].set(vec)


def augment(mat_t, vec):
    tail = jnp.zeros((SUB, S), jnp.float32).at[0].set(vec)
    return jnp.concatenate([mat_t, tail], axis=0)


def after(outer, inner):
    bias = jnp.concatenate([jnp.zeros((inner.shape[0] - SUB, S), jnp.float32), outer[S:]], axis=0)
    return jnp.dot(inner, outer[:S], precision=HIGHEST) + bias


def z_pairs(dist, src_planes):
    return [
        (tm_id(z, y, 0), tm_id(z - dist, y, 0)) for z in src_planes for y in range(NY)
    ]


def pack(carry):
    cols = carry[:64]
    state = carry[64:]
    high = lax.reduce_precision(state, 8, 7)
    low = state - high
    return jnp.concatenate([cols, high, low], axis=0).astype(jnp.bfloat16)


def unpack(packed):
    wide = packed.astype(jnp.float32)
    return jnp.concatenate([wide[:64], wide[64:72] + wide[72:80]], axis=0)


def shards(
    gain, offset, sub_offset, terminal_state, terminal_factor, obs_rows, obs_count, obs_step
):
    core = lax.axis_index("core")
    z = lax.axis_index("z")
    y = lax.axis_index("y")
    x = lax.axis_index("col")
    width = S // NX
    eye = augment(jnp.eye(S, dtype=jnp.float32), jnp.zeros((S,), jnp.float32))

    own_t = gain[0].T
    full_t = lax.all_to_all(jnp.broadcast_to(own_t, (NX, width, S)), "col", 0, 0).reshape(S, S)
    own = augment(full_t, offset[0])
    other = lax.ppermute(own, "core", [(0, 1), (1, 0)])
    first = jnp.where(core == 0, own, other)
    second = jnp.where(core == 0, other, own)
    pair = after(first, second)

    pairs = lax.all_to_all(jnp.broadcast_to(pair, (NY, AUG, S)), "y", 0, 0)
    tail2 = after(pairs[2], pairs[3])
    tail3 = after(pairs[1], tail2)
    plane = after(pairs[0], tail3)

    next_plane = lax.ppermute(plane, TM, z_pairs(1, range(1, NZ)))
    next_plane = jnp.where(z < NZ - 1, next_plane, eye)
    two = after(plane, next_plane)
    next_two = lax.ppermute(two, TM, z_pairs(2, range(2, NZ)))
    next_two = jnp.where(z < NZ - 2, next_two, eye)
    four = after(two, next_two)
    three = after(next_plane, next_two)

    term_cols = lax.dynamic_slice_in_dim(terminal_factor, x * width, width, 1).T
    top = augment(term_cols, terminal_state)
    carry = after(four, top)
    reached = top
    for step in range(1, 4):
        lo = NZ - 4 * (step + 1)
        sent = lax.ppermute(pack(carry), TM, z_pairs(4, range(lo + 4, lo + 8)))
        got = unpack(sent)
        here = jnp.logical_and(z >= lo, z < lo + 4)
        reached = jnp.where(here, got, reached)
        if step < 3:
            carry = jnp.where(here, after(four, got), carry)
    entry = pack(after(three, reached))
    crossed = lax.ppermute(entry, "core", [(0, 1)])
    entry = unpack(jnp.where(core == 0, entry, crossed))

    beyond = jnp.where(y == 0, tail3, jnp.where(y == 1, tail2, jnp.where(y == 2, pairs[3], eye)))
    group = after(jnp.where(core == 0, pair, own), beyond)
    final = after(group, entry)
    factor_t = final[:width].astype(jnp.bfloat16)
    states = (final[width][None, :] + sub_offset[0]).astype(jnp.bfloat16)

    rows_t = obs_rows.T
    pieces = [rows_t] + [
        lax.ppermute(rows_t, "col", [(i, (i + s) % NX) for i in range(NX)]) for s in (1, 2, 3)
    ]
    all_rows = jnp.zeros((S, rows_t.shape[1]), jnp.bfloat16)
    for s in range(NX):
        at = lax.rem(x - s + NX, NX) * width
        all_rows = lax.dynamic_update_slice_in_dim(all_rows, pieces[s], at, 0)

    picks = jnp.dot(states, all_rows, preferred_element_type=jnp.float32)
    onehot = obs_step[None, :] == jnp.arange(SUB)[:, None]
    guess = jnp.sum(jnp.where(onehot, picks, jnp.float32(0.0)), axis=0)
    projected = jnp.dot(factor_t, all_rows, preferred_element_type=jnp.float32)
    spread = lax.psum(jnp.sum(projected * projected, axis=0), "col")
    live = (jnp.arange(rows_t.shape[1]) < obs_count[0]).astype(jnp.float32)
    return (guess * live, spread * live)


def solution(mesh):
    torus = Mesh(mesh.devices.reshape(NZ, NY, NC, NX), ("z", "y", "core", "col"))
    in_specs = (
        P(TM, None, "col"),
        P(TM, None),
        P(TM, None, None),
        P(),
        P(),
        P(TM, "col"),
        P(TM),
        P(TM),
    )
    out_specs = (P(TM), P(TM))
    return jax.shard_map(
        shards, mesh=torus, in_specs=in_specs, out_specs=out_specs, check_vma=False
    )
```

time: 201 us -> 109 us (0.54)
  the two profiles are of different devices: /device:TPU:48 before, /device:TPU:64 now
where the time goes in v1:
time: 109 us
  blocking collectives  39.7 us (36%)
  waiting for transfers between devices  38.7 us (36%)
  starting transfers between devices  19.9 us (18%)
  matrix products  4.87 us (4%)
  other arithmetic  2.08 us (2%)
  between operations  2.01 us (2%)
  local copies, waits for them, and re-layouts  1.39 us (1%)
    ppermute x3, waiting for transfers between devices, shards(): sent = lax.ppermute(pack(carry), TM, z_pairs(4, range(lo + 4, lo + 8)))  27.4 us
    all_to_all x1, blocking collectives, shards(): pairs = lax.all_to_all(jnp.broadcast_to(pair, (NY, AUG, S)), 'y', 0, 0)  20 us
    all_to_all x1, blocking collectives, shards(): lax.all_to_all(jnp.broadcast_to(own_t, (NX, width, S)), 'col', 0, 0)  10.8 us
    ppermute x1, waiting for transfers between devices, shards(): next_two = lax.ppermute(two, TM, z_pairs(2, range(2, NZ)))  9.3 us
    ppermute x3, starting transfers between devices, shards(): lax.ppermute(rows_t, 'col', [(i, (i + s) % NX) for i in range(NX)])  9.17 us
    psum x1, blocking collectives, shards(): spread = lax.psum(jnp.sum(projected * projected, axis=0), 'col')  8.96 us
    dot_general x13, matrix products, after(): return jnp.dot(inner, outer[:S], precision=HIGHEST) + bias  4.46 us
    ppermute x1, starting transfers between devices, shards(): next_two = lax.ppermute(two, TM, z_pairs(2, range(2, NZ)))  2.9 us
  transfers between devices with their start and end apart: 10, of which 4 were waited for; matrix products, arithmetic and copies ran while one was open for 2% of the time, Pallas kernels for 0%

profile of v1, /device:TPU:64, one launch (start us, length us, event | category | flops | bytes accessed | tf_op | source)
XLA Modules:
  0.0 108.7 jit_solution(14446223690256743512)
XLA Ops:
  0.6 0.0 copy-start
  0.6 0.0 copy-start.2
  0.7 0.9 broadcast_in_dim.16
  1.6 10.8 %all_to_all.10 = f32[4,64,256]{2,1,0:T(8,128)S(1)} all-to-all(f32[4,64,256]{2,1,0:T(8,128)S(1)} %broadcast_in_dim.16), channel_id=1, replica_groups=mesh['z'=16,'y'=4,'core'=2,'col'=4] {'col'}, dimensions={0} | all-to-all | bytes 524288 | tf_op jit(solution)/shard_map/all_to_all | solution.py:62
  12.3 0.7 select_maximum_fusion
  13.0 1.9 %collective-permute-start = (f32[264,256]{1,0:T(8,128)S(1)}, f32[264,256]{1,0:T(8,128)S(1)}, u32[]{:S(2)}, u32[]{:S(2)}) collective-permute-start(f32[264,256]{1,0:T(8,128)S(1)} %select_maximum_fusion), channel_id=1, source_target_pairs={{0,4},{4,0},{1,5},{5,1},{2,6},{6,2},{3,7},{7,3},{8,12},{12,8},{9,1... | collective-permute-start | bytes 811016 | tf_op jit(solution)/shard_map/ppermute | solution.py:64
  15.0 1.5 %collective-permute-done = f32[264,256]{1,0:T(8,128)S(1)} collective-permute-done((f32[264,256]{1,0:T(8,128)S(1)}, f32[264,256]{1,0:T(8,128)S(1)}, u32[]{:S(2)}, u32[]{:S(2)}) %collective-permute-start) | collective-permute-done | bytes 270368 | tf_op jit(solution)/shard_map/ppermute | solution.py:64
  16.5 0.4 broadcast_select_fusion
  16.9 0.1 broadcast_in_dim.17
  17.0 20.0 %all_to_all.11 = f32[4,264,256]{2,1,0:T(8,128)S(1)} all-to-all(f32[4,264,256]{2,1,0:T(8,128)S(1)} %broadcast_in_dim.17), channel_id=1, replica_groups=mesh['z'=16,'y'=4,'core'=2,'col'=4] {'y'}, dimensions={0} | all-to-all | bytes 2162688 | tf_op jit(solution)/shard_map/all_to_all | solution.py:69
  37.0 0.4 convolution_add_fusion.6
  37.4 0.4 convolution_add_fusion.5
  37.8 0.4 convolution_add_fusion.4
  38.2 2.0 %collective-permute-start.1 = (f32[264,256]{1,0:T(8,128)S(1)}, f32[264,256]{1,0:T(8,128)S(1)}, u32[]{:S(2)}, u32[]{:S(2)}) collective-permute-start(f32[264,256]{1,0:T(8,128)S(1)} %convolution_add_fusion.4), channel_id=1, source_target_pairs={{32,0},{40,8},{48,16},{56,24},{64,32},{72,40},{80,48},{88,56},{96,... | collective-permute-start | bytes 811016 | tf_op jit(solution)/shard_map/ppermute | solution.py:74
  40.3 2.5 %collective-permute-start.7 = (bf16[64,1024]{1,0:T(8,128)(2,1)S(1)}, bf16[64,1024]{1,0:T(8,128)(2,1)S(1)}, u32[]{:S(2)}, u32[]{:S(2)}) collective-permute-start(bf16[64,1024]{1,0:T(8,128)(2,1)S(1)} %bitcast.48), channel_id=1, source_target_pairs={{0,1},{1,2},{2,3},{3,0},{4,5},{5,6},{6,7},{7,4},{8,9},{9,10},{10,1... | collective-permute-start | bytes 393224 | tf_op jit(solution)/shard_map/ppermute | solution.py:106
  42.7 4.0 %collective-permute-start.8 = (bf16[64,1024]{1,0:T(8,128)(2,1)S(1)}, bf16[64,1024]{1,0:T(8,128)(2,1)S(1)}, u32[]{:S(2)}, u32[]{:S(2)}) collective-permute-start(bf16[64,1024]{1,0:T(8,128)(2,1)S(1)} %bitcast.49), channel_id=1, source_target_pairs={{0,2},{1,3},{2,0},{3,1},{4,6},{5,7},{6,4},{7,5},{8,10},{9,11},{10,... | collective-permute-start | bytes 393224 | tf_op jit(solution)/shard_map/ppermute | solution.py:106
  46.7 2.7 %collective-permute-start.9 = (bf16[64,1024]{1,0:T(8,128)(2,1)S(1)}, bf16[64,1024]{1,0:T(8,128)(2,1)S(1)}, u32[]{:S(2)}, u32[]{:S(2)}) collective-permute-start(bf16[64,1024]{1,0:T(8,128)(2,1)S(1)} %bitcast.50), channel_id=1, source_target_pairs={{0,3},{1,0},{2,1},{3,2},{4,7},{5,4},{6,5},{7,6},{8,11},{9,8},{10,9... | collective-permute-start | bytes 393224 | tf_op jit(solution)/shard_map/ppermute | solution.py:106
  49.5 0.1 constant_dynamic-slice_fusion
  49.6 0.1 copy.11
  50.4 0.0 collective-permute-done.1
  50.5 0.4 convolution_add_fusion.3
  50.9 0.0 copy-start.5
  50.9 2.9 %collective-permute-start.2 = (f32[264,256]{1,0:T(8,128)S(1)}, f32[264,256]{1,0:T(8,128)S(1)}, u32[]{:S(2)}, u32[]{:S(2)}) collective-permute-start(f32[264,256]{1,0:T(8,128)S(1)} %convolution_add_fusion.3), channel_id=1, source_target_pairs={{64,0},{72,8},{80,16},{88,24},{96,32},{104,40},{112,48},{120,56},{... | collective-permute-start | bytes 811016 | tf_op jit(solution)/shard_map/ppermute | solution.py:77
  53.8 0.1 broadcast_in_dim.18
  53.9 9.3 %collective-permute-done.2 = f32[264,256]{1,0:T(8,128)S(1)} collective-permute-done((f32[264,256]{1,0:T(8,128)S(1)}, f32[264,256]{1,0:T(8,128)S(1)}, u32[]{:S(2)}, u32[]{:S(2)}) %collective-permute-start.2) | collective-permute-done | bytes 270368 | tf_op jit(solution)/shard_map/ppermute | solution.py:77
  63.2 0.4 convolution_add_fusion.2
  63.7 0.3 convolution_add_fusion.11
  64.0 0.7 collective-permute-start.3
  64.6 0.0 collective-permute-done.8
  64.7 0.3 fusion.2
  65.0 0.7 collective-permute-start.4
  65.7 0.0 collective-permute-done.4
  65.8 0.3 fusion.1
  66.1 1.3 %collective-permute-start.5 = (bf16[80,256]{1,0:T(8,128)(2,1)S(1)}, bf16[80,256]{1,0:T(8,128)(2,1)S(1)}, u32[]{:S(2)}, u32[]{:S(2)}) collective-permute-start(bf16[80,256]{1,0:T(8,128)(2,1)S(1)} %pad_maximum_fusion.8), channel_id=1, source_target_pairs={{128,0},{136,8},{144,16},{152,24},{160,32},{168,40},{176,48},{184,... | collective-permute-start | bytes 122888 | tf_op jit(solution)/shard_map/ppermute | solution.py:88
  67.4 0.4 convolution_add_fusion.1
  67.8 27.4 %collective-permute-done.5 = bf16[80,256]{1,0:T(8,128)(2,1)S(1)} collective-permute-done((bf16[80,256]{1,0:T(8,128)(2,1)S(1)}, bf16[80,256]{1,0:T(8,128)(2,1)S(1)}, u32[]{:S(2)}, u32[]{:S(2)}) %collective-permute-start.5) | collective-permute-done | bytes 40992 | tf_op jit(solution)/shard_map/ppermute | solution.py:88
  95.3 0.3 fusion.28
  95.6 0.0 copy-start.3
  95.6 0.0 copy-start.4
  95.6 1.3 %collective-permute-start.6 = (bf16[80,256]{1,0:T(8,128)(2,1)S(1)}, bf16[80,256]{1,0:T(8,128)(2,1)S(1)}, u32[]{:S(2)}, u32[]{:S(2)}) collective-permute-start(bf16[80,256]{1,0:T(8,128)(2,1)S(1)} %pad_maximum_fusion.9), channel_id=1, source_target_pairs={{0,4},{1,5},{2,6},{3,7},{8,12},{9,13},{10,14},{11,15},{16,20},{17,... | collective-permute-start | bytes 122888 | tf_op jit(solution)/shard_map/ppermute | solution.py:95
  96.9 0.4 convolution_add_fusion
  97.4 0.4 collective-permute-done.6
  97.8 0.2 convolution_add_fusion.8
  98.1 0.2 fusion
  98.3 9.0 %psum.7 = f32[1024]{0:T(1024)S(1)} all-reduce(f32[1024]{0:T(1024)S(1)} %fusion), channel_id=1, replica_groups=mesh['z'=16,'y'=4,'core'=2,'col'=4] {'col'}, use_global_device_ids=true, to_apply=%region_2.3 | all-reduce | flops 1024 | bytes 8192 | tf_op jit(solution)/shard_map/psum | solution.py:117
  107.3 0.2 fusion.3
  107.5 0.6 fusion.53
  108.1 0.6 fusion.52
  (51 shorter events, 0.4 us)
Async XLA Ops:
  0.6 48.9 %copy-start = (f32[256,256]{1,0:T(8,128)S(1)}, f32[256,256]{1,0:T(8,128)}, u32[]{:S(2)}) copy-start(f32[256,256]{1,0:T(8,128)} %param.18) | copy-start | bytes 786436
  0.6 15.8 %copy-start.2 = (f32[1,256]{1,0:T(1,128)S(1)}, f32[1,256]{1,0:T(1,128)}, u32[]{:S(2)}) copy-start(f32[1,256]{1,0:T(1,128)} %param.15) | copy-start | bytes 3076
  13.0 3.4 %collective-permute-start = (f32[264,256]{1,0:T(8,128)S(1)}, f32[264,256]{1,0:T(8,128)S(1)}, u32[]{:S(2)}, u32[]{:S(2)}) collective-permute-start(f32[264,256]{1,0:T(8,128)S(1)} %select_maximum_fusion), channel_id=1, source_target_pairs={{0,4},{4,0},{1,5},{5,1},{2,6},{6,2},{3,7},{7,3},{8,12},{12,8},{9,1... | collective-permute-start | bytes 811016 | tf_op jit(solution)/shard_map/ppermute | solution.py:64
  37.0 3.2 %copy-start.1 = (bf16[1024,64]{0,1:T(8,128)(2,1)S(1)}, bf16[1024,64]{0,1:T(8,128)(2,1)}, u32[]{:S(2)}) copy-start(bf16[1024,64]{0,1:T(8,128)(2,1)} %param.19) | copy-start | bytes 393220
  38.2 12.2 %collective-permute-start.1 = (f32[264,256]{1,0:T(8,128)S(1)}, f32[264,256]{1,0:T(8,128)S(1)}, u32[]{:S(2)}, u32[]{:S(2)}) collective-permute-start(f32[264,256]{1,0:T(8,128)S(1)} %convolution_add_fusion.4), channel_id=1, source_target_pairs={{32,0},{40,8},{48,16},{56,24},{64,32},{72,40},{80,48},{88,56},{96,... | collective-permute-start | bytes 811016 | tf_op jit(solution)/shard_map/ppermute | solution.py:74
  40.3 13.6 %collective-permute-start.7 = (bf16[64,1024]{1,0:T(8,128)(2,1)S(1)}, bf16[64,1024]{1,0:T(8,128)(2,1)S(1)}, u32[]{:S(2)}, u32[]{:S(2)}) collective-permute-start(bf16[64,1024]{1,0:T(8,128)(2,1)S(1)} %bitcast.48), channel_id=1, source_target_pairs={{0,1},{1,2},{2,3},{3,0},{4,5},{5,6},{6,7},{7,4},{8,9},{9,10},{10,1... | collective-permute-start | bytes 393224 | tf_op jit(solution)/shard_map/ppermute | solution.py:106
  42.7 21.9 %collective-permute-start.8 = (bf16[64,1024]{1,0:T(8,128)(2,1)S(1)}, bf16[64,1024]{1,0:T(8,128)(2,1)S(1)}, u32[]{:S(2)}, u32[]{:S(2)}) collective-permute-start(bf16[64,1024]{1,0:T(8,128)(2,1)S(1)} %bitcast.49), channel_id=1, source_target_pairs={{0,2},{1,3},{2,0},{3,1},{4,6},{5,7},{6,4},{7,5},{8,10},{9,11},{10,... | collective-permute-start | bytes 393224 | tf_op jit(solution)/shard_map/ppermute | solution.py:106
  46.7 19.0 %collective-permute-start.9 = (bf16[64,1024]{1,0:T(8,128)(2,1)S(1)}, bf16[64,1024]{1,0:T(8,128)(2,1)S(1)}, u32[]{:S(2)}, u32[]{:S(2)}) collective-permute-start(bf16[64,1024]{1,0:T(8,128)(2,1)S(1)} %bitcast.50), channel_id=1, source_target_pairs={{0,3},{1,0},{2,1},{3,2},{4,7},{5,4},{6,5},{7,6},{8,11},{9,8},{10,9... | collective-permute-start | bytes 393224 | tf_op jit(solution)/shard_map/ppermute | solution.py:106
  50.9 12.8 %copy-start.5 = (f32[256]{0:T(256)S(1)}, f32[256]{0:T(256)}, u32[]{:S(2)}) copy-start(f32[256]{0:T(256)} %param.17) | copy-start | bytes 3076
  50.9 12.3 %collective-permute-start.2 = (f32[264,256]{1,0:T(8,128)S(1)}, f32[264,256]{1,0:T(8,128)S(1)}, u32[]{:S(2)}, u32[]{:S(2)}) collective-permute-start(f32[264,256]{1,0:T(8,128)S(1)} %convolution_add_fusion.3), channel_id=1, source_target_pairs={{64,0},{72,8},{80,16},{88,24},{96,32},{104,40},{112,48},{120,56},{... | collective-permute-start | bytes 811016 | tf_op jit(solution)/shard_map/ppermute | solution.py:77
  64.0 0.7 collective-permute-start.3
  65.0 0.7 collective-permute-start.4
  66.1 29.1 %collective-permute-start.5 = (bf16[80,256]{1,0:T(8,128)(2,1)S(1)}, bf16[80,256]{1,0:T(8,128)(2,1)S(1)}, u32[]{:S(2)}, u32[]{:S(2)}) collective-permute-start(bf16[80,256]{1,0:T(8,128)(2,1)S(1)} %pad_maximum_fusion.8), channel_id=1, source_target_pairs={{128,0},{136,8},{144,16},{152,24},{160,32},{168,40},{176,48},{184,... | collective-permute-start | bytes 122888 | tf_op jit(solution)/shard_map/ppermute | solution.py:88
  95.6 11.7 %copy-start.3 = (f32[1,8,256]{2,1,0:T(8,128)S(1)}, f32[1,8,256]{2,1,0:T(8,128)}, u32[]{:S(2)}) copy-start(f32[1,8,256]{2,1,0:T(8,128)} %param.16) | copy-start | bytes 24580
  95.6 11.7 %copy-start.4 = (s32[1024]{0:T(1024)S(1)}, s32[1024]{0:T(1024)}, u32[]{:S(2)}) copy-start(s32[1024]{0:T(1024)} %param.21) | copy-start | bytes 12292
  95.6 2.2 %collective-permute-start.6 = (bf16[80,256]{1,0:T(8,128)(2,1)S(1)}, bf16[80,256]{1,0:T(8,128)(2,1)S(1)}, u32[]{:S(2)}, u32[]{:S(2)}) collective-permute-start(bf16[80,256]{1,0:T(8,128)(2,1)S(1)} %pad_maximum_fusion.9), channel_id=1, source_target_pairs={{0,4},{1,5},{2,6},{3,7},{8,12},{9,13},{10,14},{11,15},{16,20},{17,... | collective-permute-start | bytes 122888 | tf_op jit(solution)/shard_map/ppermute | solution.py:95

commit v2 on v1

v2 whole, which is shorter than its diff:
```python
import jax
import jax.numpy as jnp
from jax import lax
from jax.sharding import Mesh, PartitionSpec as P

S = 256
SUB = 8
NZ, NY, NC, NX = 16, 4, 2, 4
WIDTH = S // NX
TM = ("z", "y", "core")
FINE = lax.Precision.HIGH


def tm_id(z, y, c):
    return (z * NY + y) * NC + c


def along_z(moves):
    return [(tm_id(a, y, 0), tm_id(b, y, 0)) for a, b in moves for y in range(NY)]


def tail_rows(vec):
    return jnp.zeros((SUB, S), jnp.float32).at[0].set(vec)


def after(outer, inner):
    rows = inner.shape[0] - SUB
    bias = jnp.concatenate([jnp.zeros((rows, S), jnp.float32), outer[S:]], axis=0)
    return jnp.dot(inner, outer[:S], precision=FINE) + bias


def pack(carry):
    state = carry[WIDTH:]
    high = lax.reduce_precision(state, 8, 7)
    low = state - high
    return jnp.concatenate([carry[:WIDTH], high, low], axis=0).astype(jnp.bfloat16)


def unpack(packed):
    wide = packed.astype(jnp.float32)
    state = wide[WIDTH : WIDTH + SUB] + wide[WIDTH + SUB :]
    return jnp.concatenate([wide[:WIDTH], state], axis=0)


def maps_of(raw, y):
    block = raw[y * NX : (y + 1) * NX, :WIDTH].reshape(S, S)
    return jnp.concatenate([block, raw[y * NX, WIDTH:]], axis=0)


def shards(
    gain, offset, sub_offset, terminal_state, terminal_factor, obs_rows, obs_count, obs_step
):
    core = lax.axis_index("core")
    z = lax.axis_index("z")
    y = lax.axis_index("y")
    x = lax.axis_index("col")
    place = lax.rem(z, 4)
    eye = jnp.eye(S + SUB, S, dtype=jnp.float32)

    own = jnp.concatenate([gain[0].T, tail_rows(offset[0])], axis=0)
    own = lax.all_to_all(
        jnp.broadcast_to(own, (NY * NX, WIDTH + SUB, S)), ("y", "col"), 0, 0
    )
    other = lax.ppermute(own, "core", [(0, 1), (1, 0)])
    even = jnp.where(core == 0, own, other)
    odd = jnp.where(core == 0, other, own)
    pairs = [after(maps_of(even, i), maps_of(odd, i)) for i in range(NY)]
    tail2 = after(pairs[2], pairs[3])
    tail3 = after(pairs[1], tail2)
    plane = after(pairs[0], tail3)

    near = lax.ppermute(
        plane, TM, along_z([(b + j + 1, b + j) for b in range(0, NZ, 4) for j in range(3)])
    )
    near = jnp.where(place == 3, eye, near)
    two = after(plane, near)
    far0 = lax.ppermute(two, TM, along_z([(b + 2, b) for b in range(0, NZ, 4)]))
    far1 = lax.ppermute(two, TM, along_z([(b + 3, b + 1) for b in range(0, NZ, 4)]))
    far = jnp.where(place == 0, far0, jnp.where(place == 1, far1, eye))
    whole = after(two, far0)
    inside = after(near, far)

    term_cols = lax.dynamic_slice_in_dim(terminal_factor, x * WIDTH, WIDTH, 1).T
    top = jnp.concatenate([term_cols, tail_rows(terminal_state)], axis=0)
    head12 = pack(after(whole, top))
    at8 = lax.ppermute(head12, TM, along_z([(12, 8)]))
    head8 = pack(after(whole, unpack(at8)))
    at4 = lax.ppermute(head8, TM, along_z([(8, 4)]))
    head4 = pack(after(whole, unpack(at4)))
    head = jnp.where(z == 12, head12, jnp.where(z == 8, head8, head4))
    at0 = lax.ppermute(head, TM, along_z([(4, 0)]))
    fans = [
        lax.ppermute(head, TM, along_z([(b + 4, b + j) for b in (0, 4, 8)])) for j in (1, 2, 3)
    ]
    reached = jnp.where(z == 8, at8, jnp.where(z == 4, at4, at0))
    for j in (1, 2, 3):
        reached = jnp.where(place == j, fans[j - 1], reached)
    reached = jnp.where(z >= 12, top, unpack(reached))
    entry = pack(after(inside, reached))
    crossed = lax.ppermute(entry, "core", [(0, 1)])
    entry = unpack(jnp.where(core == 0, entry, crossed))

    beyond = jnp.where(
        y == 0, tail3, jnp.where(y == 1, tail2, jnp.where(y == 2, pairs[3], eye))
    )
    mine = jnp.where(y == 0, pairs[0], jnp.where(y == 1, pairs[1], jnp.where(y == 2, pairs[2], pairs[3])))
    lone = jnp.concatenate(
        [
            lax.dynamic_slice_in_dim(odd, y * NX, NX, 0)[:, :WIDTH].reshape(S, S),
            lax.dynamic_slice_in_dim(odd, y * NX, 1, 0)[0, WIDTH:],
        ],
        axis=0,
    )
    group = after(jnp.where(core == 0, mine, lone), beyond)
    final = after(group, entry)
    factor_t = final[:WIDTH].astype(jnp.bfloat16)
    states = (final[WIDTH][None, :] + sub_offset[0]).astype(jnp.bfloat16)

    rows_t = obs_rows.T
    swapped = lax.ppermute(rows_t, "col", [(0, 1), (1, 0), (2, 3), (3, 2)])
    low = lax.rem(x, 2) == 0
    half = jnp.concatenate(
        [jnp.where(low, rows_t, swapped), jnp.where(low, swapped, rows_t)], axis=0
    )
    crossed_half = lax.ppermute(half, "col", [(0, 2), (2, 0), (1, 3), (3, 1)])
    low = x < 2
    all_rows = jnp.concatenate(
        [jnp.where(low, half, crossed_half), jnp.where(low, crossed_half, half)], axis=0
    )

    picks = jnp.dot(states, all_rows, preferred_element_type=jnp.float32)
    onehot = obs_step[None, :] == jnp.arange(SUB)[:, None]
    guess = jnp.sum(jnp.where(onehot, picks, jnp.float32(0.0)), axis=0)
    projected = jnp.dot(factor_t, all_rows, preferred_element_type=jnp.float32)
    spread = lax.psum(jnp.sum(projected * projected, axis=0), "col")
    live = (jnp.arange(rows_t.shape[1]) < obs_count[0]).astype(jnp.float32)
    return (guess * live, spread * live)


def solution(mesh):
    torus = Mesh(mesh.devices.reshape(NZ, NY, NC, NX), ("z", "y", "core", "col"))
    in_specs = (
        P(TM, None, "col"),
        P(TM, None),
        P(TM, None, None),
        P(),
        P(),
        P(TM, "col"),
        P(TM),
        P(TM),
    )
    out_specs = (P(TM), P(TM))
    return jax.shard_map(
        shards, mesh=torus, in_specs=in_specs, out_specs=out_specs, check_vma=False
    )
```

time: 109 us -> 101 us (0.927)
  the two profiles are of different devices: /device:TPU:64 before, /device:TPU:2 now
where the time goes in v2:
time: 101 us
  waiting for transfers between devices  39.4 us (39%)
  blocking collectives  33.7 us (33%)
  starting transfers between devices  17.6 us (17%)
  matrix products  4.71 us (5%)
  other arithmetic  2.57 us (3%)
  between operations  2.03 us (2%)
    all_to_all x1, blocking collectives, shards(): lax.all_to_all(jnp.broadcast_to(own, (NY * NX, WIDTH + SUB, S)), ('y', 'c...  24.6 us
    ppermute x1, waiting for transfers between devices, shards(): at0 = lax.ppermute(head, TM, along_z([(4, 0)]))  19.8 us
    psum x1, blocking collectives, shards(): spread = lax.psum(jnp.sum(projected * projected, axis=0), 'col')  9.19 us
    ppermute x1, waiting for transfers between devices, shards(): far0 = lax.ppermute(two, TM, along_z([(b + 2, b) for b in range(0, NZ, 4)]))  7.01 us
    ppermute x1, waiting for transfers between devices, shards(): crossed_half = lax.ppermute(half, 'col', [(0, 2), (2, 0), (1, 3), (3, 1)])  5.64 us
    dot_general x16, matrix products, after(): return jnp.dot(inner, outer[:S], precision=FINE) + bias  4.3 us
    ppermute x1, waiting for transfers between devices, shards(): lax.ppermute(plane, TM, along_z([(b + j + 1, b + j) for b in range(0, NZ,...  3.59 us
    ppermute x1, starting transfers between devices, shards(): swapped = lax.ppermute(rows_t, 'col', [(0, 1), (1, 0), (2, 3), (3, 2)])  3.43 us
  transfers between devices with their start and end apart: 13, of which 6 were waited for; matrix products, arithmetic and copies ran while one was open for 2% of the time, Pallas kernels for 0%

profile of v2, /device:TPU:2, one launch (start us, length us, event | category | flops | bytes accessed | tf_op | source)
XLA Modules:
  0.0 100.6 jit_solution(639517943199085583)
XLA Ops:
  0.6 0.9 select_maximum_fusion
  1.6 0.1 broadcast_in_dim.9
  1.6 24.6 %all_to_all.5 = f32[16,72,256]{2,1,0:T(8,128)S(1)} all-to-all(f32[16,72,256]{2,1,0:T(8,128)S(1)} %broadcast_in_dim.9), channel_id=1, replica_groups=mesh['z'=16,'y'=4,'core'=2,'col'=4] {'y','col'}, dimensions={0} | all-to-all | bytes 2359296 | tf_op jit(solution)/shard_map/all_to_all | solution.py:61
  26.2 1.9 %collective-permute-start = (f32[16,72,256]{2,1,0:T(8,128)S(1)}, f32[16,72,256]{2,1,0:T(8,128)S(1)}, u32[]{:S(2)}, u32[]{:S(2)}) collective-permute-start(f32[16,72,256]{2,1,0:T(8,128)S(1)} %all_to_all.5), channel_id=1, source_target_pairs={{0,4},{4,0},{1,5},{5,1},{2,6},{6,2},{3,7},{7,3},{8,12},{12,8},{9,1... | collective-permute-start | bytes 3538952 | tf_op jit(solution)/shard_map/ppermute | solution.py:64
  28.1 2.8 %collective-permute-done = f32[16,72,256]{2,1,0:T(8,128)S(1)} collective-permute-done((f32[16,72,256]{2,1,0:T(8,128)S(1)}, f32[16,72,256]{2,1,0:T(8,128)S(1)}, u32[]{:S(2)}, u32[]{:S(2)}) %collective-permute-start) | collective-permute-done | bytes 1179680 | tf_op jit(solution)/shard_map/ppermute | solution.py:64
  30.9 0.2 broadcast_select_fusion.1
  31.1 0.2 fusion.81
  31.3 0.3 convolution_add_fusion.9
  31.6 0.3 convolution_add_fusion.7
  31.9 0.3 convolution_add_fusion.10
  32.2 0.3 maximum_select_fusion
  32.5 0.3 convolution_add_fusion.8
  32.8 0.3 convolution_add_fusion.6
  33.1 0.3 convolution_add_fusion.4
  33.4 1.3 %collective-permute-start.1 = (f32[264,256]{1,0:T(8,128)S(1)}, f32[264,256]{1,0:T(8,128)S(1)}, u32[]{:S(2)}, u32[]{:S(2)}) collective-permute-start(f32[264,256]{1,0:T(8,128)S(1)} %convolution_add_fusion.4), channel_id=1, source_target_pairs={{32,0},{40,8},{48,16},{56,24},{64,32},{72,40},{80,48},{88,56},{96,... | collective-permute-start | bytes 811016 | tf_op jit(solution)/shard_map/ppermute | solution.py:72
  34.7 3.4 %collective-permute-start.11 = (bf16[64,1024]{1,0:T(8,128)(2,1)S(1)}, bf16[64,1024]{1,0:T(8,128)(2,1)S(1)}, u32[]{:S(2)}, u32[]{:S(2)}) collective-permute-start(bf16[64,1024]{1,0:T(8,128)(2,1)S(1)} %bitcast.64), channel_id=1, source_target_pairs={{0,1},{1,0},{2,3},{3,2},{4,5},{5,4},{6,7},{7,6},{8,9},{9,8},{10,11... | collective-permute-start | bytes 393224 | tf_op jit(solution)/shard_map/ppermute | solution.py:120
  38.2 3.6 %collective-permute-done.1 = f32[264,256]{1,0:T(8,128)S(1)} collective-permute-done((f32[264,256]{1,0:T(8,128)S(1)}, f32[264,256]{1,0:T(8,128)S(1)}, u32[]{:S(2)}, u32[]{:S(2)}) %collective-permute-start.1) | collective-permute-done | bytes 270368 | tf_op jit(solution)/shard_map/ppermute | solution.py:72
  41.8 0.3 convolution_add_fusion.3
  42.1 1.3 %collective-permute-start.2 = (f32[264,256]{1,0:T(8,128)S(1)}, f32[264,256]{1,0:T(8,128)S(1)}, u32[]{:S(2)}, u32[]{:S(2)}) collective-permute-start(f32[264,256]{1,0:T(8,128)S(1)} %convolution_add_fusion.3), channel_id=1, source_target_pairs={{64,0},{72,8},{80,16},{88,24},{192,128},{200,136},{208,144},{216,1... | collective-permute-start | bytes 811016 | tf_op jit(solution)/shard_map/ppermute | solution.py:77
  43.4 0.1 constant_dynamic-slice_fusion.1
  43.6 0.1 copy.11
  44.4 7.0 %collective-permute-done.2 = f32[264,256]{1,0:T(8,128)S(1)} collective-permute-done((f32[264,256]{1,0:T(8,128)S(1)}, f32[264,256]{1,0:T(8,128)S(1)}, u32[]{:S(2)}, u32[]{:S(2)}) %collective-permute-start.2) | collective-permute-done | bytes 270368 | tf_op jit(solution)/shard_map/ppermute | solution.py:77
  51.4 0.3 convolution_add_fusion.2
  51.7 0.2 convolution_add_fusion.14
  51.9 0.7 collective-permute-start.3
  52.6 3.1 %collective-permute-start.12 = (bf16[128,1024]{1,0:T(8,128)(2,1)S(1)}, bf16[128,1024]{1,0:T(8,128)(2,1)S(1)}, u32[]{:S(2)}, u32[]{:S(2)}) collective-permute-start(bf16[128,1024]{1,0:T(8,128)(2,1)S(1)} %pad_maximum_fusion.3), channel_id=1, source_target_pairs={{0,2},{2,0},{1,3},{3,1},{4,6},{6,4},{5,7},{7,5},{8,10},{10,8},{9,1... | collective-permute-start | bytes 786440 | tf_op jit(solution)/shard_map/ppermute | solution.py:125
  55.8 0.2 convolution_add_fusion.13
  56.1 0.7 collective-permute-start.4
  56.8 5.6 %collective-permute-done.12 = bf16[128,1024]{1,0:T(8,128)(2,1)S(1)} collective-permute-done((bf16[128,1024]{1,0:T(8,128)(2,1)S(1)}, bf16[128,1024]{1,0:T(8,128)(2,1)S(1)}, u32[]{:S(2)}, u32[]{:S(2)}) %collective-permute-start.12) | collective-permute-done | bytes 262176 | tf_op jit(solution)/shard_map/ppermute | solution.py:125
  62.4 0.1 broadcast_select_fusion.3
  62.5 0.7 collective-permute-start.9
  63.3 0.2 convolution_add_fusion.12
  63.6 0.7 collective-permute-start.5
  64.2 0.7 collective-permute-start.6
  64.9 0.7 collective-permute-start.7
  65.6 1.3 %collective-permute-start.8 = (bf16[80,256]{1,0:T(8,128)(2,1)S(1)}, bf16[80,256]{1,0:T(8,128)(2,1)S(1)}, u32[]{:S(2)}, u32[]{:S(2)}) collective-permute-start(bf16[80,256]{1,0:T(8,128)(2,1)S(1)} %fusion.51), channel_id=1, source_target_pairs={{128,0},{136,8},{144,16},{152,24},{129,1},{137,9},{145,17},{153,25... | collective-permute-start | bytes 122888 | tf_op jit(solution)/shard_map/ppermute | solution.py:91
  66.9 0.3 convolution_add_fusion.1
  67.3 19.8 %collective-permute-done.8 = bf16[80,256]{1,0:T(8,128)(2,1)S(1)} collective-permute-done((bf16[80,256]{1,0:T(8,128)(2,1)S(1)}, bf16[80,256]{1,0:T(8,128)(2,1)S(1)}, u32[]{:S(2)}, u32[]{:S(2)}) %collective-permute-start.8) | collective-permute-done | bytes 40992 | tf_op jit(solution)/shard_map/ppermute | solution.py:91
  87.1 0.2 fusion.43
  87.4 1.3 %collective-permute-start.10 = (bf16[80,256]{1,0:T(8,128)(2,1)S(1)}, bf16[80,256]{1,0:T(8,128)(2,1)S(1)}, u32[]{:S(2)}, u32[]{:S(2)}) collective-permute-start(bf16[80,256]{1,0:T(8,128)(2,1)S(1)} %pad_maximum_fusion.6), channel_id=1, source_target_pairs={{0,4},{1,5},{2,6},{3,7},{8,12},{9,13},{10,14},{11,15},{16,20},{17,... | collective-permute-start | bytes 122888 | tf_op jit(solution)/shard_map/ppermute | solution.py:100
  88.7 0.3 convolution_add_fusion
  89.0 0.5 collective-permute-done.10
  89.6 0.2 convolution_add_fusion.11
  89.8 0.2 fusion
  90.0 9.2 %psum.7 = f32[1024]{0:T(1024)S(1)} all-reduce(f32[1024]{0:T(1024)S(1)} %fusion), channel_id=1, replica_groups=mesh['z'=16,'y'=4,'core'=2,'col'=4] {'col'}, use_global_device_ids=true, to_apply=%region_2.3 | all-reduce | flops 1024 | bytes 8192 | tf_op jit(solution)/shard_map/psum | solution.py:135
  99.2 0.6 fusion.64
  99.8 0.2 fusion.1
  100.0 0.6 fusion.65
  (56 shorter events, 0.4 us)
Async XLA Ops:
  0.6 42.8 %copy-start = (f32[256,256]{1,0:T(8,128)S(1)}, f32[256,256]{1,0:T(8,128)}, u32[]{:S(2)}) copy-start(f32[256,256]{1,0:T(8,128)} %param.16) | copy-start | bytes 786436
  26.2 4.7 %collective-permute-start = (f32[16,72,256]{2,1,0:T(8,128)S(1)}, f32[16,72,256]{2,1,0:T(8,128)S(1)}, u32[]{:S(2)}, u32[]{:S(2)}) collective-permute-start(f32[16,72,256]{2,1,0:T(8,128)S(1)} %all_to_all.5), channel_id=1, source_target_pairs={{0,4},{4,0},{1,5},{5,1},{2,6},{6,2},{3,7},{7,3},{8,12},{12,8},{9,1... | collective-permute-start | bytes 3538952 | tf_op jit(solution)/shard_map/ppermute | solution.py:64
  32.5 2.2 %copy-start.1 = (bf16[1024,64]{0,1:T(8,128)(2,1)S(1)}, bf16[1024,64]{0,1:T(8,128)(2,1)}, u32[]{:S(2)}) copy-start(bf16[1024,64]{0,1:T(8,128)(2,1)} %param.17) | copy-start | bytes 393220
  33.4 8.4 %collective-permute-start.1 = (f32[264,256]{1,0:T(8,128)S(1)}, f32[264,256]{1,0:T(8,128)S(1)}, u32[]{:S(2)}, u32[]{:S(2)}) collective-permute-start(f32[264,256]{1,0:T(8,128)S(1)} %convolution_add_fusion.4), channel_id=1, source_target_pairs={{32,0},{40,8},{48,16},{56,24},{64,32},{72,40},{80,48},{88,56},{96,... | collective-permute-start | bytes 811016 | tf_op jit(solution)/shard_map/ppermute | solution.py:72
  34.7 9.6 %collective-permute-start.11 = (bf16[64,1024]{1,0:T(8,128)(2,1)S(1)}, bf16[64,1024]{1,0:T(8,128)(2,1)S(1)}, u32[]{:S(2)}, u32[]{:S(2)}) collective-permute-start(bf16[64,1024]{1,0:T(8,128)(2,1)S(1)} %bitcast.64), channel_id=1, source_target_pairs={{0,1},{1,0},{2,3},{3,2},{4,5},{5,4},{6,7},{7,6},{8,9},{9,8},{10,11... | collective-permute-start | bytes 393224 | tf_op jit(solution)/shard_map/ppermute | solution.py:120
  41.8 9.9 %copy-start.2 = (f32[256]{0:T(256)S(1)}, f32[256]{0:T(256)}, u32[]{:S(2)}) copy-start(f32[256]{0:T(256)} %param.15) | copy-start | bytes 3076
  42.1 9.3 %collective-permute-start.2 = (f32[264,256]{1,0:T(8,128)S(1)}, f32[264,256]{1,0:T(8,128)S(1)}, u32[]{:S(2)}, u32[]{:S(2)}) collective-permute-start(f32[264,256]{1,0:T(8,128)S(1)} %convolution_add_fusion.3), channel_id=1, source_target_pairs={{64,0},{72,8},{80,16},{88,24},{192,128},{200,136},{208,144},{216,1... | collective-permute-start | bytes 811016 | tf_op jit(solution)/shard_map/ppermute | solution.py:77
  51.9 3.8 %collective-permute-start.3 = (bf16[80,256]{1,0:T(8,128)(2,1)S(1)}, bf16[80,256]{1,0:T(8,128)(2,1)S(1)}, u32[]{:S(2)}, u32[]{:S(2)}) collective-permute-start(bf16[80,256]{1,0:T(8,128)(2,1)S(1)} %pad_maximum_fusion.4), channel_id=1, source_target_pairs={{384,256},{392,264},{400,272},{408,280},{385,257},{393,265},{401,2... | collective-permute-start | bytes 122888 | tf_op jit(solution)/shard_map/ppermute | solution.py:86
  52.6 9.8 %collective-permute-start.12 = (bf16[128,1024]{1,0:T(8,128)(2,1)S(1)}, bf16[128,1024]{1,0:T(8,128)(2,1)S(1)}, u32[]{:S(2)}, u32[]{:S(2)}) collective-permute-start(bf16[128,1024]{1,0:T(8,128)(2,1)S(1)} %pad_maximum_fusion.3), channel_id=1, source_target_pairs={{0,2},{2,0},{1,3},{3,1},{4,6},{6,4},{5,7},{7,5},{8,10},{10,8},{9,1... | collective-permute-start | bytes 786440 | tf_op jit(solution)/shard_map/ppermute | solution.py:125
  56.1 7.1 %collective-permute-start.4 = (bf16[80,256]{1,0:T(8,128)(2,1)S(1)}, bf16[80,256]{1,0:T(8,128)(2,1)S(1)}, u32[]{:S(2)}, u32[]{:S(2)}) collective-permute-start(bf16[80,256]{1,0:T(8,128)(2,1)S(1)} %pad_maximum_fusion.5), channel_id=1, source_target_pairs={{256,128},{264,136},{272,144},{280,152},{257,129},{265,137},{273,1... | collective-permute-start | bytes 122888 | tf_op jit(solution)/shard_map/ppermute | solution.py:88
  62.5 4.3 %collective-permute-start.9 = (f32[264,256]{1,0:T(8,128)S(1)}, f32[264,256]{1,0:T(8,128)S(1)}, u32[]{:S(2)}, u32[]{:S(2)}) collective-permute-start(f32[264,256]{1,0:T(8,128)S(1)} %convolution_add_fusion.3), channel_id=1, source_target_pairs={{96,32},{104,40},{112,48},{120,56},{224,160},{232,168},{240,176},{... | collective-permute-start | bytes 811016 | tf_op jit(solution)/shard_map/ppermute | solution.py:78
  63.6 3.7 %collective-permute-start.5 = (bf16[80,256]{1,0:T(8,128)(2,1)S(1)}, bf16[80,256]{1,0:T(8,128)(2,1)S(1)}, u32[]{:S(2)}, u32[]{:S(2)}) collective-permute-start(bf16[80,256]{1,0:T(8,128)(2,1)S(1)} %fusion.51), channel_id=1, source_target_pairs={{128,96},{136,104},{144,112},{152,120},{256,224},{264,232},{272,24... | collective-permute-start | bytes 122888 | tf_op jit(solution)/shard_map/ppermute | solution.py:93
  64.2 3.0 %collective-permute-start.6 = (bf16[80,256]{1,0:T(8,128)(2,1)S(1)}, bf16[80,256]{1,0:T(8,128)(2,1)S(1)}, u32[]{:S(2)}, u32[]{:S(2)}) collective-permute-start(bf16[80,256]{1,0:T(8,128)(2,1)S(1)} %fusion.51), channel_id=1, source_target_pairs={{128,64},{136,72},{144,80},{152,88},{256,192},{264,200},{272,208},... | collective-permute-start | bytes 122888 | tf_op jit(solution)/shard_map/ppermute | solution.py:93
  64.9 2.3 %collective-permute-start.7 = (bf16[80,256]{1,0:T(8,128)(2,1)S(1)}, bf16[80,256]{1,0:T(8,128)(2,1)S(1)}, u32[]{:S(2)}, u32[]{:S(2)}) collective-permute-start(bf16[80,256]{1,0:T(8,128)(2,1)S(1)} %fusion.51), channel_id=1, source_target_pairs={{128,32},{136,40},{144,48},{152,56},{256,160},{264,168},{272,176},... | collective-permute-start | bytes 122888 | tf_op jit(solution)/shard_map/ppermute | solution.py:93
  65.6 21.5 %collective-permute-start.8 = (bf16[80,256]{1,0:T(8,128)(2,1)S(1)}, bf16[80,256]{1,0:T(8,128)(2,1)S(1)}, u32[]{:S(2)}, u32[]{:S(2)}) collective-permute-start(bf16[80,256]{1,0:T(8,128)(2,1)S(1)} %fusion.51), channel_id=1, source_target_pairs={{128,0},{136,8},{144,16},{152,24},{129,1},{137,9},{145,17},{153,25... | collective-permute-start | bytes 122888 | tf_op jit(solution)/shard_map/ppermute | solution.py:91
  87.4 2.2 %collective-permute-start.10 = (bf16[80,256]{1,0:T(8,128)(2,1)S(1)}, bf16[80,256]{1,0:T(8,128)(2,1)S(1)}, u32[]{:S(2)}, u32[]{:S(2)}) collective-permute-start(bf16[80,256]{1,0:T(8,128)(2,1)S(1)} %pad_maximum_fusion.6), channel_id=1, source_target_pairs={{0,4},{1,5},{2,6},{3,7},{8,12},{9,13},{10,14},{11,15},{16,20},{17,... | collective-permute-start | bytes 122888 | tf_op jit(solution)/shard_map/ppermute | solution.py:100
  89.0 10.8 %copy-start.3 = (f32[1,8,256]{2,1,0:T(8,128)S(1)}, f32[1,8,256]{2,1,0:T(8,128)}, u32[]{:S(2)}) copy-start(f32[1,8,256]{2,1,0:T(8,128)} %param.14) | copy-start | bytes 24580
  89.0 10.8 %copy-start.4 = (s32[1024]{0:T(1024)S(1)}, s32[1024]{0:T(1024)}, u32[]{:S(2)}) copy-start(s32[1024]{0:T(1024)} %param.19) | copy-start | bytes 12292

commit v3 on v2

--- a/solution.py
+++ b/solution.py
@@ -3,10 +3,12 @@
 from jax import lax
 from jax.sharding import Mesh, PartitionSpec as P
 
+
 S = 256
 SUB = 8
 NZ, NY, NC, NX = 16, 4, 2, 4
 WIDTH = S // NX
+CARRY = WIDTH + SUB
 TM = ("z", "y", "core")
 FINE = lax.Precision.HIGH
 
@@ -29,17 +31,22 @@
     return jnp.dot(inner, outer[:S], precision=FINE) + bias
 
 
-def pack(carry):
-    state = carry[WIDTH:]
+def packed(cols, state):
+    row = lax.broadcasted_iota(jnp.int32, (CARRY, S), 0)
     high = lax.reduce_precision(state, 8, 7)
     low = state - high
-    return jnp.concatenate([carry[:WIDTH], high, low], axis=0).astype(jnp.bfloat16)
+    tail = jnp.where(row == WIDTH, high, jnp.where(row == WIDTH + 1, low, 0.0))
+    return jnp.where(row < WIDTH, cols, tail).astype(jnp.bfloat16)
 
 
-def unpack(packed):
-    wide = packed.astype(jnp.float32)
-    state = wide[WIDTH : WIDTH + SUB] + wide[WIDTH + SUB :]
-    return jnp.concatenate([wide[:WIDTH], state], axis=0)
+def moved(outer, carry):
+    cols = jnp.dot(carry.astype(jnp.float32), outer[:S], precision=lax.Precision.HIGHEST)
+    state = cols[WIDTH : WIDTH + 1] + cols[WIDTH + 1 : WIDTH + 2] + outer[S : S + 1]
+    return cols, state
+
+
+def hop(outer, carry):
+    return packed(*moved(outer, carry))
 
 
 def maps_of(raw, y):
@@ -47,7 +54,7 @@
     return jnp.concatenate([block, raw[y * NX, WIDTH:]], axis=0)
 
 
-def shards(
+def compute(
     gain, offset, sub_offset, terminal_state, terminal_factor, obs_rows, obs_count, obs_step
 ):
     core = lax.axis_index("core")
@@ -69,36 +76,49 @@
     tail3 = after(pairs[1], tail2)
     plane = after(pairs[0], tail3)
 
+    top_cols = lax.dynamic_slice_in_dim(terminal_factor, x * WIDTH, WIDTH, 1).T
+    top = packed(
+        jnp.concatenate([top_cols, jnp.zeros((SUB, S), jnp.float32)], axis=0), terminal_state[None, :]
+    )
+    low_blocks = (0, 4, 8)
+
     near = lax.ppermute(
-        plane, TM, along_z([(b + j + 1, b + j) for b in range(0, NZ, 4) for j in range(3)])
+        plane, TM, along_z([(b + j + 1, b + j) for b in low_blocks for j in range(3)] + [(13, 12)])
     )
-    near = jnp.where(place == 3, eye, near)
+    head15 = hop(plane, top)
+    at14 = lax.ppermute(head15, TM, along_z([(15, 14)]))
+    head14 = hop(plane, at14)
+    at12 = lax.ppermute(head14, TM, along_z([(14, 12)]))
+    near = jnp.where(jnp.logical_or(place == 3, z >= 13), eye, near)
     two = after(plane, near)
-    far0 = lax.ppermute(two, TM, along_z([(b + 2, b) for b in range(0, NZ, 4)]))
-    far1 = lax.ppermute(two, TM, along_z([(b + 3, b + 1) for b in range(0, NZ, 4)]))
-    far = jnp.where(place == 0, far0, jnp.where(place == 1, far1, eye))
+    far0 = lax.ppermute(two, TM, along_z([(b + 2, b) for b in low_blocks]))
+    head12 = hop(two, at12)
+    at8 = lax.ppermute(head12, TM, along_z([(12, 8)]))
     whole = after(two, far0)
+    head8 = hop(whole, at8)
+    at4 = lax.ppermute(head8, TM, along_z([(8, 4)]))
+    far1 = lax.ppermute(two, TM, along_z([(b + 3, b + 1) for b in low_blocks]))
+    at13 = lax.ppermute(head14, TM, along_z([(14, 13)]))
+    far = jnp.where(
+        jnp.logical_and(place == 0, z < 12),
+        far0,
+        jnp.where(jnp.logical_and(place == 1, z < 12), far1, eye),
+    )
     inside = after(near, far)
-
-    term_cols = lax.dynamic_slice_in_dim(terminal_factor, x * WIDTH, WIDTH, 1).T
-    top = jnp.concatenate([term_cols, tail_rows(terminal_state)], axis=0)
-    head12 = pack(after(whole, top))
-    at8 = lax.ppermute(head12, TM, along_z([(12, 8)]))
-    head8 = pack(after(whole, unpack(at8)))
-    at4 = lax.ppermute(head8, TM, along_z([(8, 4)]))
-    head4 = pack(after(whole, unpack(at4)))
+    head4 = hop(whole, at4)
     head = jnp.where(z == 12, head12, jnp.where(z == 8, head8, head4))
     at0 = lax.ppermute(head, TM, along_z([(4, 0)]))
-    fans = [
-        lax.ppermute(head, TM, along_z([(b + 4, b + j) for b in (0, 4, 8)])) for j in (1, 2, 3)
-    ]
+    fans = []
+    for j in (1, 2, 3):
+        fans.append(lax.ppermute(head, TM, along_z([(b + 4, b + j) for b in low_blocks])))
     reached = jnp.where(z == 8, at8, jnp.where(z == 4, at4, at0))
     for j in (1, 2, 3):
         reached = jnp.where(place == j, fans[j - 1], reached)
-    reached = jnp.where(z >= 12, top, unpack(reached))
-    entry = pack(after(inside, reached))
+    reached = jnp.where(z == 12, at12, jnp.where(z == 13, at13, jnp.where(z == 14, at14, reached)))
+    reached = jnp.where(z == 15, top, reached)
+    entry = hop(inside, reached)
     crossed = lax.ppermute(entry, "core", [(0, 1)])
-    entry = unpack(jnp.where(core == 0, entry, crossed))
+    entry = jnp.where(core == 0, entry, crossed)
 
     beyond = jnp.where(
         y == 0, tail3, jnp.where(y == 1, tail2, jnp.where(y == 2, pairs[3], eye))
@@ -112,9 +132,9 @@
         axis=0,
     )
     group = after(jnp.where(core == 0, mine, lone), beyond)
-    final = after(group, entry)
-    factor_t = final[:WIDTH].astype(jnp.bfloat16)
-    states = (final[WIDTH][None, :] + sub_offset[0]).astype(jnp.bfloat16)
+    cols, state = moved(group, entry)
+    factor_t = cols[:WIDTH].astype(jnp.bfloat16)
+    states = (state + sub_offset[0]).astype(jnp.bfloat16)
 
     rows_t = obs_rows.T
     swapped = lax.ppermute(rows_t, "col", [(0, 1), (1, 0), (2, 3), (3, 2)])
@@ -132,9 +152,12 @@
     onehot = obs_step[None, :] == jnp.arange(SUB)[:, None]
     guess = jnp.sum(jnp.where(onehot, picks, jnp.float32(0.0)), axis=0)
     projected = jnp.dot(factor_t, all_rows, preferred_element_type=jnp.float32)
-    spread = lax.psum(jnp.sum(projected * projected, axis=0), "col")
+    part = jnp.sum(projected * projected, axis=0)
     live = (jnp.arange(rows_t.shape[1]) < obs_count[0]).astype(jnp.float32)
-    return (guess * live, spread * live)
+    guess = guess * live
+    part, guess = lax.optimization_barrier((part, guess))
+    parts = lax.all_to_all(jnp.broadcast_to(part, (NX, part.shape[0])), "col", 0, 0)
+    return (guess, jnp.sum(parts, axis=0) * live)
 
 
 def solution(mesh):
@@ -151,5 +174,5 @@
     )
     out_specs = (P(TM), P(TM))
     return jax.shard_map(
-        shards, mesh=torus, in_specs=in_specs, out_specs=out_specs, check_vma=False
+        compute, mesh=torus, in_specs=in_specs, out_specs=out_specs, check_vma=False
     )

time: 101 us -> 100 us (0.990)
  the two profiles are of different devices: /device:TPU:2 before, /device:TPU:1 now
where the time goes in v3:
time: 100 us
  waiting for transfers between devices  38.2 us (38%)
  blocking collectives  31.6 us (32%)
  starting transfers between devices  19 us (19%)
  matrix products  5.34 us (5%)
  other arithmetic  3.17 us (3%)
  between operations  2.1 us (2%)
    ppermute x1, waiting for transfers between devices, compute(): crossed = lax.ppermute(entry, 'core', [(0, 1)])  31.9 us
    all_to_all x1, blocking collectives, compute(): lax.all_to_all(jnp.broadcast_to(own, (NY * NX, WIDTH + SUB, S)), ('y', 'c...  24.3 us
    all_to_all x1, blocking collectives, compute(): lax.all_to_all(jnp.broadcast_to(part, (NX, part.shape[0])), 'col', 0, 0)  7.33 us
    ppermute x1, starting transfers between devices, compute(): other = lax.ppermute(own, 'core', [(0, 1), (1, 0)])  4.77 us
    ppermute x1, waiting for transfers between devices, compute(): swapped = lax.ppermute(rows_t, 'col', [(0, 1), (1, 0), (2, 3), (3, 2)])  3.82 us
    dot_general x11, matrix products, after(): return jnp.dot(inner, outer[:S], precision=FINE) + bias  3.24 us
    ppermute x1, starting transfers between devices, compute(): crossed_half = lax.ppermute(half, 'col', [(0, 2), (2, 0), (1, 3), (3, 1)])  2.76 us
    ppermute x1, waiting for transfers between devices, compute(): crossed_half = lax.ppermute(half, 'col', [(0, 2), (2, 0), (1, 3), (3, 1)])  2.41 us
  transfers between devices with their start and end apart: 16, of which 3 were waited for; matrix products, arithmetic and copies ran while one was open for 3% of the time, Pallas kernels for 0%

profile of v3, /device:TPU:1, one launch (start us, length us, event | category | flops | bytes accessed | tf_op | source)
XLA Modules:
  0.0 100.0 jit_solution(10065464427874844182)
XLA Ops:
  0.6 0.9 select_maximum_fusion
  1.7 24.3 %all_to_all.11 = f32[16,72,256]{2,1,0:T(8,128)S(1)} all-to-all(f32[16,72,256]{2,1,0:T(8,128)S(1)} %broadcast_in_dim.126), channel_id=1, replica_groups=mesh['z'=16,'y'=4,'core'=2,'col'=4] {'y','col'}, dimensions={0} | all-to-all | bytes 2359296 | tf_op jit(solution)/shard_map/all_to_all | solution.py:68
  26.0 4.8 %collective-permute-start = (f32[16,72,256]{2,1,0:T(8,128)S(1)}, f32[16,72,256]{2,1,0:T(8,128)S(1)}, u32[]{:S(2)}, u32[]{:S(2)}) collective-permute-start(f32[16,72,256]{2,1,0:T(8,128)S(1)} %all_to_all.11), channel_id=1, source_target_pairs={{0,4},{4,0},{1,5},{5,1},{2,6},{6,2},{3,7},{7,3},{8,12},{12,8},{9,1... | collective-permute-start | bytes 3538952 | tf_op jit(solution)/shard_map/ppermute | solution.py:71
  30.7 2.1 %collective-permute-start.14 = (bf16[64,1024]{1,0:T(8,128)(2,1)S(1)}, bf16[64,1024]{1,0:T(8,128)(2,1)S(1)}, u32[]{:S(2)}, u32[]{:S(2)}) collective-permute-start(bf16[64,1024]{1,0:T(8,128)(2,1)S(1)} %bitcast.77), channel_id=1, source_target_pairs={{0,1},{1,0},{2,3},{3,2},{4,5},{5,4},{6,7},{7,6},{8,9},{9,8},{10,11... | collective-permute-start | bytes 393224 | tf_op jit(solution)/shard_map/ppermute | solution.py:140
  33.9 3.8 %collective-permute-done.14 = bf16[64,1024]{1,0:T(8,128)(2,1)S(1)} collective-permute-done((bf16[64,1024]{1,0:T(8,128)(2,1)S(1)}, bf16[64,1024]{1,0:T(8,128)(2,1)S(1)}, u32[]{:S(2)}, u32[]{:S(2)}) %collective-permute-start.14) | collective-permute-done | bytes 131104 | tf_op jit(solution)/shard_map/ppermute | solution.py:140
  37.7 0.2 broadcast_select_fusion.1
  37.9 0.3 fusion.92
  38.2 0.3 convolution_add_fusion.9
  38.5 0.3 convolution_add_fusion.7
  38.8 0.3 convolution_add_fusion.10
  39.1 0.3 maximum_select_fusion
  39.5 0.3 convolution_add_fusion.8
  39.7 0.3 convolution_add_fusion.6
  40.0 0.3 convolution_add_fusion.4
  40.3 0.2 fusion.38
  40.7 0.7 collective-permute-start.1
  41.4 2.8 %collective-permute-start.15 = (bf16[128,1024]{1,0:T(8,128)(2,1)S(1)}, bf16[128,1024]{1,0:T(8,128)(2,1)S(1)}, u32[]{:S(2)}, u32[]{:S(2)}) collective-permute-start(bf16[128,1024]{1,0:T(8,128)(2,1)S(1)} %pad_maximum_fusion.3), channel_id=1, source_target_pairs={{0,2},{2,0},{1,3},{3,1},{4,6},{6,4},{5,7},{7,5},{8,10},{10,8},{9,1... | collective-permute-start | bytes 786440 | tf_op jit(solution)/shard_map/ppermute | solution.py:145
  44.2 0.7 collective-permute-start.4
  44.9 0.2 fusion.36
  45.3 0.7 collective-permute-start.2
  46.0 0.3 convolution_add_fusion.3
  46.3 0.7 collective-permute-start.6
  47.0 0.2 fusion.33
  47.4 0.7 collective-permute-start.5
  48.0 0.3 convolution_add_fusion.2
  48.3 0.2 fusion.30
  48.7 0.7 collective-permute-start.7
  49.4 2.4 %collective-permute-done.15 = bf16[128,1024]{1,0:T(8,128)(2,1)S(1)} collective-permute-done((bf16[128,1024]{1,0:T(8,128)(2,1)S(1)}, bf16[128,1024]{1,0:T(8,128)(2,1)S(1)}, u32[]{:S(2)}, u32[]{:S(2)}) %collective-permute-start.15) | collective-permute-done | bytes 262176 | tf_op jit(solution)/shard_map/ppermute | solution.py:145
  51.8 0.1 broadcast_select_fusion.3
  51.9 0.7 collective-permute-start.3
  52.6 0.7 collective-permute-start.12
  53.3 0.2 fusion.28
  53.6 0.1 fusion.46
  53.7 0.7 collective-permute-start.10
  54.4 0.7 collective-permute-start.11
  55.0 0.7 collective-permute-start.8
  55.7 0.7 collective-permute-start.9
  56.4 0.3 convolution_add_fusion.1
  56.7 0.3 fusion.22
  57.2 1.3 %collective-permute-start.13 = (bf16[72,256]{1,0:T(8,128)(2,1)S(1)}, bf16[72,256]{1,0:T(8,128)(2,1)S(1)}, u32[]{:S(2)}, u32[]{:S(2)}) collective-permute-start(bf16[72,256]{1,0:T(8,128)(2,1)S(1)} %select_convert_fusion), channel_id=1, source_target_pairs={{0,4},{1,5},{2,6},{3,7},{8,12},{9,13},{10,14},{11,15},{16,20},{17,... | collective-permute-start | bytes 110600 | tf_op jit(solution)/shard_map/ppermute | solution.py:120
  58.5 0.3 convolution_add_fusion
  58.8 31.9 %collective-permute-done.13 = bf16[72,256]{1,0:T(8,128)(2,1)S(1)} collective-permute-done((bf16[72,256]{1,0:T(8,128)(2,1)S(1)}, bf16[72,256]{1,0:T(8,128)(2,1)S(1)}, u32[]{:S(2)}, u32[]{:S(2)}) %collective-permute-start.13) | collective-permute-done | bytes 36896 | tf_op jit(solution)/shard_map/ppermute | solution.py:120
  90.8 0.2 fusion.19
  91.0 0.2 fusion
  91.3 0.2 fusion.1
  91.5 0.6 fusion.71
  92.1 7.3 %all_to_all.12 = f32[4,1,1024]{2,1,0:T(1,128)S(1)} all-to-all(f32[4,1,1024]{2,1,0:T(1,128)S(1)} %broadcast_in_dim.152), channel_id=1, replica_groups=mesh['z'=16,'y'=4,'core'=2,'col'=4] {'col'}, dimensions={0} | all-to-all | bytes 32768 | tf_op jit(solution)/shard_map/all_to_all | solution.py:159
  99.4 0.6 fusion.70
  (60 shorter events, 1.1 us)
Async XLA Ops:
  0.6 32.3 %copy-start = (f32[256,256]{1,0:T(8,128)S(1)}, f32[256,256]{1,0:T(8,128)}, u32[]{:S(2)}) copy-start(f32[256,256]{1,0:T(8,128)} %param.14) | copy-start | bytes 786436
  1.6 29.1 %copy-start.1 = (bf16[1024,64]{0,1:T(8,128)(2,1)S(1)}, bf16[1024,64]{0,1:T(8,128)(2,1)}, u32[]{:S(2)}) copy-start(bf16[1024,64]{0,1:T(8,128)(2,1)} %param.15) | copy-start | bytes 393220
  1.6 31.4 %copy-start.2 = (f32[256]{0:T(256)S(1)}, f32[256]{0:T(256)}, u32[]{:S(2)}) copy-start(f32[256]{0:T(256)} %param.13) | copy-start | bytes 3076
  26.0 11.8 %collective-permute-start = (f32[16,72,256]{2,1,0:T(8,128)S(1)}, f32[16,72,256]{2,1,0:T(8,128)S(1)}, u32[]{:S(2)}, u32[]{:S(2)}) collective-permute-start(f32[16,72,256]{2,1,0:T(8,128)S(1)} %all_to_all.11), channel_id=1, source_target_pairs={{0,4},{4,0},{1,5},{5,1},{2,6},{6,2},{3,7},{7,3},{8,12},{12,8},{9,1... | collective-permute-start | bytes 3538952 | tf_op jit(solution)/shard_map/ppermute | solution.py:71
  30.7 6.9 %collective-permute-start.14 = (bf16[64,1024]{1,0:T(8,128)(2,1)S(1)}, bf16[64,1024]{1,0:T(8,128)(2,1)S(1)}, u32[]{:S(2)}, u32[]{:S(2)}) collective-permute-start(bf16[64,1024]{1,0:T(8,128)(2,1)S(1)} %bitcast.77), channel_id=1, source_target_pairs={{0,1},{1,0},{2,3},{3,2},{4,5},{5,4},{6,7},{7,6},{8,9},{9,8},{10,11... | collective-permute-start | bytes 393224 | tf_op jit(solution)/shard_map/ppermute | solution.py:140
  40.7 4.2 %collective-permute-start.1 = (bf16[72,256]{1,0:T(8,128)(2,1)S(1)}, bf16[72,256]{1,0:T(8,128)(2,1)S(1)}, u32[]{:S(2)}, u32[]{:S(2)}) collective-permute-start(bf16[72,256]{1,0:T(8,128)(2,1)S(1)} %select_convert_fusion.5), channel_id=1, source_target_pairs={{480,448},{488,456},{496,464},{504,472},{481,449},{489,457},{497,4... | collective-permute-start | bytes 110600 | tf_op jit(solution)/shard_map/ppermute | solution.py:89
  41.4 10.4 %collective-permute-start.15 = (bf16[128,1024]{1,0:T(8,128)(2,1)S(1)}, bf16[128,1024]{1,0:T(8,128)(2,1)S(1)}, u32[]{:S(2)}, u32[]{:S(2)}) collective-permute-start(bf16[128,1024]{1,0:T(8,128)(2,1)S(1)} %pad_maximum_fusion.3), channel_id=1, source_target_pairs={{0,2},{2,0},{1,3},{3,1},{4,6},{6,4},{5,7},{7,5},{8,10},{10,8},{9,1... | collective-permute-start | bytes 786440 | tf_op jit(solution)/shard_map/ppermute | solution.py:145
  44.2 1.7 %collective-permute-start.4 = (f32[264,256]{1,0:T(8,128)S(1)}, f32[264,256]{1,0:T(8,128)S(1)}, u32[]{:S(2)}, u32[]{:S(2)}) collective-permute-start(f32[264,256]{1,0:T(8,128)S(1)} %convolution_add_fusion.4), channel_id=1, source_target_pairs={{32,0},{40,8},{48,16},{56,24},{64,32},{72,40},{80,48},{88,56},{96,... | collective-permute-start | bytes 811016 | tf_op jit(solution)/shard_map/ppermute | solution.py:85
  45.3 1.7 %collective-permute-start.2 = (bf16[72,256]{1,0:T(8,128)(2,1)S(1)}, bf16[72,256]{1,0:T(8,128)(2,1)S(1)}, u32[]{:S(2)}, u32[]{:S(2)}) collective-permute-start(bf16[72,256]{1,0:T(8,128)(2,1)S(1)} %select_convert_fusion.4), channel_id=1, source_target_pairs={{448,384},{456,392},{464,400},{472,408},{449,385},{457,393},{465,4... | collective-permute-start | bytes 110600 | tf_op jit(solution)/shard_map/ppermute | solution.py:91
  46.3 1.8 %collective-permute-start.6 = (f32[264,256]{1,0:T(8,128)S(1)}, f32[264,256]{1,0:T(8,128)S(1)}, u32[]{:S(2)}, u32[]{:S(2)}) collective-permute-start(f32[264,256]{1,0:T(8,128)S(1)} %convolution_add_fusion.3), channel_id=1, source_target_pairs={{64,0},{72,8},{80,16},{88,24},{192,128},{200,136},{208,144},{216,1... | collective-permute-start | bytes 811016 | tf_op jit(solution)/shard_map/ppermute | solution.py:94
  47.4 1.0 collective-permute-start.5
  48.7 4.6 %collective-permute-start.7 = (bf16[72,256]{1,0:T(8,128)(2,1)S(1)}, bf16[72,256]{1,0:T(8,128)(2,1)S(1)}, u32[]{:S(2)}, u32[]{:S(2)}) collective-permute-start(bf16[72,256]{1,0:T(8,128)(2,1)S(1)} %select_convert_fusion.2), channel_id=1, source_target_pairs={{256,128},{264,136},{272,144},{280,152},{257,129},{265,137},{273,1... | collective-permute-start | bytes 110600 | tf_op jit(solution)/shard_map/ppermute | solution.py:99
  51.9 4.8 %collective-permute-start.3 = (bf16[72,256]{1,0:T(8,128)(2,1)S(1)}, bf16[72,256]{1,0:T(8,128)(2,1)S(1)}, u32[]{:S(2)}, u32[]{:S(2)}) collective-permute-start(bf16[72,256]{1,0:T(8,128)(2,1)S(1)} %select_convert_fusion.4), channel_id=1, source_target_pairs={{448,416},{456,424},{464,432},{472,440},{449,417},{457,425},{465,4... | collective-permute-start | bytes 110600 | tf_op jit(solution)/shard_map/ppermute | solution.py:101
  52.6 3.1 %collective-permute-start.12 = (f32[264,256]{1,0:T(8,128)S(1)}, f32[264,256]{1,0:T(8,128)S(1)}, u32[]{:S(2)}, u32[]{:S(2)}) collective-permute-start(f32[264,256]{1,0:T(8,128)S(1)} %convolution_add_fusion.3), channel_id=1, source_target_pairs={{96,32},{104,40},{112,48},{120,56},{224,160},{232,168},{240,176},{... | collective-permute-start | bytes 811016 | tf_op jit(solution)/shard_map/ppermute | solution.py:100
  53.7 3.0 %collective-permute-start.10 = (bf16[72,256]{1,0:T(8,128)(2,1)S(1)}, bf16[72,256]{1,0:T(8,128)(2,1)S(1)}, u32[]{:S(2)}, u32[]{:S(2)}) collective-permute-start(bf16[72,256]{1,0:T(8,128)(2,1)S(1)} %fusion.46), channel_id=1, source_target_pairs={{128,32},{136,40},{144,48},{152,56},{256,160},{264,168},{272,176},... | collective-permute-start | bytes 110600 | tf_op jit(solution)/shard_map/ppermute | solution.py:113
  54.4 2.4 %collective-permute-start.11 = (bf16[72,256]{1,0:T(8,128)(2,1)S(1)}, bf16[72,256]{1,0:T(8,128)(2,1)S(1)}, u32[]{:S(2)}, u32[]{:S(2)}) collective-permute-start(bf16[72,256]{1,0:T(8,128)(2,1)S(1)} %fusion.46), channel_id=1, source_target_pairs={{128,0},{136,8},{144,16},{152,24},{129,1},{137,9},{145,17},{153,25... | collective-permute-start | bytes 110600 | tf_op jit(solution)/shard_map/ppermute | solution.py:110
  55.0 1.7 %collective-permute-start.8 = (bf16[72,256]{1,0:T(8,128)(2,1)S(1)}, bf16[72,256]{1,0:T(8,128)(2,1)S(1)}, u32[]{:S(2)}, u32[]{:S(2)}) collective-permute-start(bf16[72,256]{1,0:T(8,128)(2,1)S(1)} %fusion.46), channel_id=1, source_target_pairs={{128,96},{136,104},{144,112},{152,120},{256,224},{264,232},{272,24... | collective-permute-start | bytes 110600 | tf_op jit(solution)/shard_map/ppermute | solution.py:113
  55.7 1.0 %collective-permute-start.9 = (bf16[72,256]{1,0:T(8,128)(2,1)S(1)}, bf16[72,256]{1,0:T(8,128)(2,1)S(1)}, u32[]{:S(2)}, u32[]{:S(2)}) collective-permute-start(bf16[72,256]{1,0:T(8,128)(2,1)S(1)} %fusion.46), channel_id=1, source_target_pairs={{128,64},{136,72},{144,80},{152,88},{256,192},{264,200},{272,208},... | collective-permute-start | bytes 110600 | tf_op jit(solution)/shard_map/ppermute | solution.py:113
  57.2 34.1 %copy-start.3 = (f32[1,8,256]{2,1,0:T(8,128)S(1)}, f32[1,8,256]{2,1,0:T(8,128)}, u32[]{:S(2)}) copy-start(f32[1,8,256]{2,1,0:T(8,128)} %param.12) | copy-start | bytes 24580
  57.2 34.1 %copy-start.4 = (s32[1024]{0:T(1024)S(1)}, s32[1024]{0:T(1024)}, u32[]{:S(2)}) copy-start(s32[1024]{0:T(1024)} %param.17) | copy-start | bytes 12292
  57.2 33.6 %collective-permute-start.13 = (bf16[72,256]{1,0:T(8,128)(2,1)S(1)}, bf16[72,256]{1,0:T(8,128)(2,1)S(1)}, u32[]{:S(2)}, u32[]{:S(2)}) collective-permute-start(bf16[72,256]{1,0:T(8,128)(2,1)S(1)} %select_convert_fusion), channel_id=1, source_target_pairs={{0,4},{1,5},{2,6},{3,7},{8,12},{9,13},{10,14},{11,15},{16,20},{17,... | collective-permute-start | bytes 110600 | tf_op jit(solution)/shard_map/ppermute | solution.py:120

commit v4 on v3

--- a/solution.py
+++ b/solution.py
@@ -83,17 +83,19 @@
     low_blocks = (0, 4, 8)
 
     near = lax.ppermute(
-        plane, TM, along_z([(b + j + 1, b + j) for b in low_blocks for j in range(3)] + [(13, 12)])
+        plane, TM, along_z([(b + j + 1, b + j) for b in low_blocks for j in range(3)])
     )
+    near12 = lax.ppermute(plane, TM, along_z([(13, 12)]))
     head15 = hop(plane, top)
     at14 = lax.ppermute(head15, TM, along_z([(15, 14)]))
     head14 = hop(plane, at14)
     at12 = lax.ppermute(head14, TM, along_z([(14, 12)]))
-    near = jnp.where(jnp.logical_or(place == 3, z >= 13), eye, near)
+    two12 = after(plane, near12)
+    head12 = hop(two12, at12)
+    at8 = lax.ppermute(head12, TM, along_z([(12, 8)]))
+    near = jnp.where(place == 3, eye, near)
     two = after(plane, near)
     far0 = lax.ppermute(two, TM, along_z([(b + 2, b) for b in low_blocks]))
-    head12 = hop(two, at12)
-    at8 = lax.ppermute(head12, TM, along_z([(12, 8)]))
     whole = after(two, far0)
     head8 = hop(whole, at8)
     at4 = lax.ppermute(head8, TM, along_z([(8, 4)]))
@@ -104,7 +106,7 @@
         far0,
         jnp.where(jnp.logical_and(place == 1, z < 12), far1, eye),
     )
-    inside = after(near, far)
+    inside = jnp.where(z > 12, eye, jnp.where(z == 12, near12, after(near, far)))
     head4 = hop(whole, at4)
     head = jnp.where(z == 12, head12, jnp.where(z == 8, head8, head4))
     at0 = lax.ppermute(head, TM, along_z([(4, 0)]))
@@ -154,10 +156,9 @@
     projected = jnp.dot(factor_t, all_rows, preferred_element_type=jnp.float32)
     part = jnp.sum(projected * projected, axis=0)
     live = (jnp.arange(rows_t.shape[1]) < obs_count[0]).astype(jnp.float32)
-    guess = guess * live
-    part, guess = lax.optimization_barrier((part, guess))
     parts = lax.all_to_all(jnp.broadcast_to(part, (NX, part.shape[0])), "col", 0, 0)
-    return (guess, jnp.sum(parts, axis=0) * live)
+    spread = (parts[0] + parts[1]) + (parts[2] + parts[3])
+    return (guess * live, spread * live)
 
 
 def solution(mesh):

time: 100 us -> 102 us (1.020)
  blocking collectives: 31.6 us -> 24.3 us
  starting transfers between devices: 19 us -> 23 us
  waiting for transfers between devices: 38.2 us -> 42.2 us
    all_to_all x1 -> x0, blocking collectives: 7.33 us -> none  [compute(): lax.all_to_all(jnp.broadcast_to(part, (NX, part.shape[0])), 'col', 0, 0)]
    all_to_all x0 -> x1, waiting for transfers between devices: none -> 3.41 us  [compute(): lax.all_to_all(jnp.broadcast_to(part, (NX, part.shape[0])), 'col', 0, 0)]
    all_to_all x0 -> x1, starting transfers between devices: none -> 3.33 us  [compute(): lax.all_to_all(jnp.broadcast_to(part, (NX, part.shape[0])), 'col', 0, 0)]
    ppermute x1, waiting for transfers between devices: 31.9 us -> 33.5 us  [compute(): crossed = lax.ppermute(entry, 'core', [(0, 1)])]
    dot_general x11 -> x12, matrix products: 3.24 us -> 3.51 us  [after(): return jnp.dot(inner, outer[:S], precision=FINE) + bias]
  transfers between devices with their start and end apart: 16 -> 18, of which waited for: 3 -> 4; matrix products, arithmetic and copies ran while one was open for 3% -> 4% of each run, Pallas kernels for 0% -> 0%
where the time goes in v4:
time: 102 us
  waiting for transfers between devices  42.2 us (41%)
  blocking collectives  24.3 us (24%)
  starting transfers between devices  23 us (23%)
  matrix products  5.61 us (6%)
  other arithmetic  3.16 us (3%)
  between operations  2.1 us (2%)
  local copies, waits for them, and re-layouts  1.23 us (1%)
    ppermute x1, waiting for transfers between devices, compute(): crossed = lax.ppermute(entry, 'core', [(0, 1)])  33.5 us
    all_to_all x1, blocking collectives, compute(): lax.all_to_all(jnp.broadcast_to(own, (NY * NX, WIDTH + SUB, S)), ('y', 'c...  24.3 us
    ppermute x1, starting transfers between devices, compute(): other = lax.ppermute(own, 'core', [(0, 1), (1, 0)])  4.77 us
    ppermute x1, waiting for transfers between devices, compute(): swapped = lax.ppermute(rows_t, 'col', [(0, 1), (1, 0), (2, 3), (3, 2)])  3.83 us
    dot_general x12, matrix products, after(): return jnp.dot(inner, outer[:S], precision=FINE) + bias  3.51 us
    all_to_all x1, waiting for transfers between devices, compute(): lax.all_to_all(jnp.broadcast_to(part, (NX, part.shape[0])), 'col', 0, 0)  3.41 us
    all_to_all x1, starting transfers between devices, compute(): lax.all_to_all(jnp.broadcast_to(part, (NX, part.shape[0])), 'col', 0, 0)  3.33 us
    ppermute x1, starting transfers between devices, compute(): crossed_half = lax.ppermute(half, 'col', [(0, 2), (2, 0), (1, 3), (3, 1)])  2.76 us
  transfers between devices with their start and end apart: 18, of which 4 were waited for; matrix products, arithmetic and copies ran while one was open for 4% of the time, Pallas kernels for 0%

profile of v4, /device:TPU:1, one launch (start us, length us, event | category | flops | bytes accessed | tf_op | source)
XLA Modules:
  0.0 101.6 jit_solution(14675745865669078651)
XLA Ops:
  0.6 0.9 select_maximum_fusion
  1.7 24.3 %all_to_all.11 = f32[16,72,256]{2,1,0:T(8,128)S(1)} all-to-all(f32[16,72,256]{2,1,0:T(8,128)S(1)} %broadcast_in_dim.126), channel_id=1, replica_groups=mesh['z'=16,'y'=4,'core'=2,'col'=4] {'y','col'}, dimensions={0} | all-to-all | bytes 2359296 | tf_op jit(solution)/shard_map/all_to_all | solution.py:68
  26.0 4.8 %collective-permute-start = (f32[16,72,256]{2,1,0:T(8,128)S(1)}, f32[16,72,256]{2,1,0:T(8,128)S(1)}, u32[]{:S(2)}, u32[]{:S(2)}) collective-permute-start(f32[16,72,256]{2,1,0:T(8,128)S(1)} %all_to_all.11), channel_id=1, source_target_pairs={{0,4},{4,0},{1,5},{5,1},{2,6},{6,2},{3,7},{7,3},{8,12},{12,8},{9,1... | collective-permute-start | bytes 3538952 | tf_op jit(solution)/shard_map/ppermute | solution.py:71
  30.7 2.1 %collective-permute-start.15 = (bf16[64,1024]{1,0:T(8,128)(2,1)S(1)}, bf16[64,1024]{1,0:T(8,128)(2,1)S(1)}, u32[]{:S(2)}, u32[]{:S(2)}) collective-permute-start(bf16[64,1024]{1,0:T(8,128)(2,1)S(1)} %bitcast.79), channel_id=1, source_target_pairs={{0,1},{1,0},{2,3},{3,2},{4,5},{5,4},{6,7},{7,6},{8,9},{9,8},{10,11... | collective-permute-start | bytes 393224 | tf_op jit(solution)/shard_map/ppermute | solution.py:142
  33.9 3.8 %collective-permute-done.15 = bf16[64,1024]{1,0:T(8,128)(2,1)S(1)} collective-permute-done((bf16[64,1024]{1,0:T(8,128)(2,1)S(1)}, bf16[64,1024]{1,0:T(8,128)(2,1)S(1)}, u32[]{:S(2)}, u32[]{:S(2)}) %collective-permute-start.15) | collective-permute-done | bytes 131104 | tf_op jit(solution)/shard_map/ppermute | solution.py:142
  37.9 0.3 fusion.96
  38.2 0.3 convolution_add_fusion.10
  38.5 0.3 convolution_add_fusion.8
  38.8 0.3 convolution_add_fusion.11
  39.1 0.3 maximum_select_fusion
  39.4 0.3 convolution_add_fusion.9
  39.7 0.3 convolution_add_fusion.7
  40.0 0.3 convolution_add_fusion.5
  40.3 0.2 fusion.41
  40.7 0.7 collective-permute-start.1
  41.4 2.8 %collective-permute-start.16 = (bf16[128,1024]{1,0:T(8,128)(2,1)S(1)}, bf16[128,1024]{1,0:T(8,128)(2,1)S(1)}, u32[]{:S(2)}, u32[]{:S(2)}) collective-permute-start(bf16[128,1024]{1,0:T(8,128)(2,1)S(1)} %pad_maximum_fusion.3), channel_id=1, source_target_pairs={{0,2},{2,0},{1,3},{3,1},{4,6},{6,4},{5,7},{7,5},{8,10},{10,8},{9,1... | collective-permute-start | bytes 786440 | tf_op jit(solution)/shard_map/ppermute | solution.py:147
  44.2 0.7 collective-permute-start.6
  44.9 0.7 collective-permute-start.4
  45.6 0.2 fusion.39
  45.9 0.7 collective-permute-start.2
  46.7 0.3 convolution_add_fusion.3
  46.9 0.7 collective-permute-start.7
  47.6 0.3 convolution_add_fusion.4
  48.0 0.2 fusion.28
  48.3 0.7 collective-permute-start.5
  49.0 0.3 convolution_add_fusion.2
  49.3 0.2 fusion.35
  49.7 0.7 collective-permute-start.8
  50.4 1.4 %collective-permute-done.16 = bf16[128,1024]{1,0:T(8,128)(2,1)S(1)} collective-permute-done((bf16[128,1024]{1,0:T(8,128)(2,1)S(1)}, bf16[128,1024]{1,0:T(8,128)(2,1)S(1)}, u32[]{:S(2)}, u32[]{:S(2)}) %collective-permute-start.16) | collective-permute-done | bytes 262176 | tf_op jit(solution)/shard_map/ppermute | solution.py:147
  51.9 0.7 collective-permute-start.3
  52.6 0.7 collective-permute-start.13
  53.3 0.2 fusion.33
  53.7 0.7 collective-permute-start.10
  54.4 0.7 collective-permute-start.11
  55.0 0.7 collective-permute-start.12
  55.7 0.7 collective-permute-start.9
  56.4 0.3 fusion.1
  56.7 0.3 fusion.24
  57.2 1.3 %collective-permute-start.14 = (bf16[72,256]{1,0:T(8,128)(2,1)S(1)}, bf16[72,256]{1,0:T(8,128)(2,1)S(1)}, u32[]{:S(2)}, u32[]{:S(2)}) collective-permute-start(bf16[72,256]{1,0:T(8,128)(2,1)S(1)} %select_convert_fusion), channel_id=1, source_target_pairs={{0,4},{1,5},{2,6},{3,7},{8,12},{9,13},{10,14},{11,15},{16,20},{17,... | collective-permute-start | bytes 110600 | tf_op jit(solution)/shard_map/ppermute | solution.py:122
  58.5 0.3 convolution_add_fusion
  58.8 33.5 %collective-permute-done.14 = bf16[72,256]{1,0:T(8,128)(2,1)S(1)} collective-permute-done((bf16[72,256]{1,0:T(8,128)(2,1)S(1)}, bf16[72,256]{1,0:T(8,128)(2,1)S(1)}, u32[]{:S(2)}, u32[]{:S(2)}) %collective-permute-start.14) | collective-permute-done | bytes 36896 | tf_op jit(solution)/shard_map/ppermute | solution.py:122
  92.3 0.2 fusion.21
  92.6 0.2 fusion.2
  92.8 0.6 broadcast_in_dim.152
  93.4 3.3 %all-to-all-start.1 = ((f32[4,1,1024]{2,1,0:T(1,128)}), f32[4,1,1024]{2,1,0:T(1,128)S(1)}, u32[]{:S(2)}, u32[]{:S(2)}) async-start(f32[4,1,1024]{2,1,0:T(1,128)} %broadcast_in_dim.152), calls=%async_computation.1 | async-start | bytes 32768 | tf_op jit(solution)/shard_map/all_to_all | solution.py:159
  97.0 0.6 fusion.75
  97.6 3.4 %all-to-all-done.1 = f32[4,1,1024]{2,1,0:T(1,128)S(1)} async-done(((f32[4,1,1024]{2,1,0:T(1,128)}), f32[4,1,1024]{2,1,0:T(1,128)S(1)}, u32[]{:S(2)}, u32[]{:S(2)}) %all-to-all-start.1) | async-done | bytes 16416 | tf_op jit(solution)/shard_map/all_to_all | solution.py:159
  101.0 0.6 fusion.74
  (64 shorter events, 1.6 us)
Async XLA Ops:
  0.6 32.3 %copy-start = (f32[256,256]{1,0:T(8,128)S(1)}, f32[256,256]{1,0:T(8,128)}, u32[]{:S(2)}) copy-start(f32[256,256]{1,0:T(8,128)} %param.14) | copy-start | bytes 786436
  1.6 29.1 %copy-start.1 = (bf16[1024,64]{0,1:T(8,128)(2,1)S(1)}, bf16[1024,64]{0,1:T(8,128)(2,1)}, u32[]{:S(2)}) copy-start(bf16[1024,64]{0,1:T(8,128)(2,1)} %param.15) | copy-start | bytes 393220
  1.6 31.4 %copy-start.2 = (f32[256]{0:T(256)S(1)}, f32[256]{0:T(256)}, u32[]{:S(2)}) copy-start(f32[256]{0:T(256)} %param.13) | copy-start | bytes 3076
  26.0 11.8 %collective-permute-start = (f32[16,72,256]{2,1,0:T(8,128)S(1)}, f32[16,72,256]{2,1,0:T(8,128)S(1)}, u32[]{:S(2)}, u32[]{:S(2)}) collective-permute-start(f32[16,72,256]{2,1,0:T(8,128)S(1)} %all_to_all.11), channel_id=1, source_target_pairs={{0,4},{4,0},{1,5},{5,1},{2,6},{6,2},{3,7},{7,3},{8,12},{12,8},{9,1... | collective-permute-start | bytes 3538952 | tf_op jit(solution)/shard_map/ppermute | solution.py:71
  30.7 6.9 %collective-permute-start.15 = (bf16[64,1024]{1,0:T(8,128)(2,1)S(1)}, bf16[64,1024]{1,0:T(8,128)(2,1)S(1)}, u32[]{:S(2)}, u32[]{:S(2)}) collective-permute-start(bf16[64,1024]{1,0:T(8,128)(2,1)S(1)} %bitcast.79), channel_id=1, source_target_pairs={{0,1},{1,0},{2,3},{3,2},{4,5},{5,4},{6,7},{7,6},{8,9},{9,8},{10,11... | collective-permute-start | bytes 393224 | tf_op jit(solution)/shard_map/ppermute | solution.py:142
  40.7 4.9 %collective-permute-start.1 = (bf16[72,256]{1,0:T(8,128)(2,1)S(1)}, bf16[72,256]{1,0:T(8,128)(2,1)S(1)}, u32[]{:S(2)}, u32[]{:S(2)}) collective-permute-start(bf16[72,256]{1,0:T(8,128)(2,1)S(1)} %select_convert_fusion.5), channel_id=1, source_target_pairs={{480,448},{488,456},{496,464},{504,472},{481,449},{489,457},{497,4... | collective-permute-start | bytes 110600 | tf_op jit(solution)/shard_map/ppermute | solution.py:90
  41.4 10.4 %collective-permute-start.16 = (bf16[128,1024]{1,0:T(8,128)(2,1)S(1)}, bf16[128,1024]{1,0:T(8,128)(2,1)S(1)}, u32[]{:S(2)}, u32[]{:S(2)}) collective-permute-start(bf16[128,1024]{1,0:T(8,128)(2,1)S(1)} %pad_maximum_fusion.3), channel_id=1, source_target_pairs={{0,2},{2,0},{1,3},{3,1},{4,6},{6,4},{5,7},{7,5},{8,10},{10,8},{9,1... | collective-permute-start | bytes 786440 | tf_op jit(solution)/shard_map/ppermute | solution.py:147
  44.2 2.4 %collective-permute-start.6 = (f32[264,256]{1,0:T(8,128)S(1)}, f32[264,256]{1,0:T(8,128)S(1)}, u32[]{:S(2)}, u32[]{:S(2)}) collective-permute-start(f32[264,256]{1,0:T(8,128)S(1)} %convolution_add_fusion.5), channel_id=1, source_target_pairs={{32,0},{40,8},{48,16},{56,24},{64,32},{72,40},{80,48},{88,56},{96,... | collective-permute-start | bytes 811016 | tf_op jit(solution)/shard_map/ppermute | solution.py:85
  44.9 2.8 %collective-permute-start.4 = (f32[264,256]{1,0:T(8,128)S(1)}, f32[264,256]{1,0:T(8,128)S(1)}, u32[]{:S(2)}, u32[]{:S(2)}) collective-permute-start(f32[264,256]{1,0:T(8,128)S(1)} %convolution_add_fusion.5), channel_id=1, source_target_pairs={{416,384},{424,392},{432,400},{440,408},{417,385},{425,393},{433,4... | collective-permute-start | bytes 811016 | tf_op jit(solution)/shard_map/ppermute | solution.py:88
  45.9 2.0 %collective-permute-start.2 = (bf16[72,256]{1,0:T(8,128)(2,1)S(1)}, bf16[72,256]{1,0:T(8,128)(2,1)S(1)}, u32[]{:S(2)}, u32[]{:S(2)}) collective-permute-start(bf16[72,256]{1,0:T(8,128)(2,1)S(1)} %select_convert_fusion.4), channel_id=1, source_target_pairs={{448,384},{456,392},{464,400},{472,408},{449,385},{457,393},{465,4... | collective-permute-start | bytes 110600 | tf_op jit(solution)/shard_map/ppermute | solution.py:92
  46.9 2.1 %collective-permute-start.7 = (f32[264,256]{1,0:T(8,128)S(1)}, f32[264,256]{1,0:T(8,128)S(1)}, u32[]{:S(2)}, u32[]{:S(2)}) collective-permute-start(f32[264,256]{1,0:T(8,128)S(1)} %convolution_add_fusion.3), channel_id=1, source_target_pairs={{64,0},{72,8},{80,16},{88,24},{192,128},{200,136},{208,144},{216,1... | collective-permute-start | bytes 811016 | tf_op jit(solution)/shard_map/ppermute | solution.py:98
  48.3 1.0 collective-permute-start.5
  49.7 3.6 %collective-permute-start.8 = (bf16[72,256]{1,0:T(8,128)(2,1)S(1)}, bf16[72,256]{1,0:T(8,128)(2,1)S(1)}, u32[]{:S(2)}, u32[]{:S(2)}) collective-permute-start(bf16[72,256]{1,0:T(8,128)(2,1)S(1)} %select_convert_fusion.2), channel_id=1, source_target_pairs={{256,128},{264,136},{272,144},{280,152},{257,129},{265,137},{273,1... | collective-permute-start | bytes 110600 | tf_op jit(solution)/shard_map/ppermute | solution.py:101
  51.9 4.8 %collective-permute-start.3 = (bf16[72,256]{1,0:T(8,128)(2,1)S(1)}, bf16[72,256]{1,0:T(8,128)(2,1)S(1)}, u32[]{:S(2)}, u32[]{:S(2)}) collective-permute-start(bf16[72,256]{1,0:T(8,128)(2,1)S(1)} %select_convert_fusion.4), channel_id=1, source_target_pairs={{448,416},{456,424},{464,432},{472,440},{449,417},{457,425},{465,4... | collective-permute-start | bytes 110600 | tf_op jit(solution)/shard_map/ppermute | solution.py:103
  52.6 3.1 %collective-permute-start.13 = (f32[264,256]{1,0:T(8,128)S(1)}, f32[264,256]{1,0:T(8,128)S(1)}, u32[]{:S(2)}, u32[]{:S(2)}) collective-permute-start(f32[264,256]{1,0:T(8,128)S(1)} %convolution_add_fusion.3), channel_id=1, source_target_pairs={{96,32},{104,40},{112,48},{120,56},{224,160},{232,168},{240,176},{... | collective-permute-start | bytes 811016 | tf_op jit(solution)/shard_map/ppermute | solution.py:102
  53.7 3.0 %collective-permute-start.10 = (bf16[72,256]{1,0:T(8,128)(2,1)S(1)}, bf16[72,256]{1,0:T(8,128)(2,1)S(1)}, u32[]{:S(2)}, u32[]{:S(2)}) collective-permute-start(bf16[72,256]{1,0:T(8,128)(2,1)S(1)} %fusion.49), channel_id=1, source_target_pairs={{128,64},{136,72},{144,80},{152,88},{256,192},{264,200},{272,208},... | collective-permute-start | bytes 110600 | tf_op jit(solution)/shard_map/ppermute | solution.py:115
  54.4 2.4 %collective-permute-start.11 = (bf16[72,256]{1,0:T(8,128)(2,1)S(1)}, bf16[72,256]{1,0:T(8,128)(2,1)S(1)}, u32[]{:S(2)}, u32[]{:S(2)}) collective-permute-start(bf16[72,256]{1,0:T(8,128)(2,1)S(1)} %fusion.49), channel_id=1, source_target_pairs={{128,32},{136,40},{144,48},{152,56},{256,160},{264,168},{272,176},... | collective-permute-start | bytes 110600 | tf_op jit(solution)/shard_map/ppermute | solution.py:115
  55.0 1.7 %collective-permute-start.12 = (bf16[72,256]{1,0:T(8,128)(2,1)S(1)}, bf16[72,256]{1,0:T(8,128)(2,1)S(1)}, u32[]{:S(2)}, u32[]{:S(2)}) collective-permute-start(bf16[72,256]{1,0:T(8,128)(2,1)S(1)} %fusion.49), channel_id=1, source_target_pairs={{128,0},{136,8},{144,16},{152,24},{129,1},{137,9},{145,17},{153,25... | collective-permute-start | bytes 110600 | tf_op jit(solution)/shard_map/ppermute | solution.py:112
  55.7 1.0 %collective-permute-start.9 = (bf16[72,256]{1,0:T(8,128)(2,1)S(1)}, bf16[72,256]{1,0:T(8,128)(2,1)S(1)}, u32[]{:S(2)}, u32[]{:S(2)}) collective-permute-start(bf16[72,256]{1,0:T(8,128)(2,1)S(1)} %fusion.49), channel_id=1, source_target_pairs={{128,96},{136,104},{144,112},{152,120},{256,224},{264,232},{272,24... | collective-permute-start | bytes 110600 | tf_op jit(solution)/shard_map/ppermute | solution.py:115
  57.2 39.6 %copy-start.3 = (f32[1,8,256]{2,1,0:T(8,128)S(1)}, f32[1,8,256]{2,1,0:T(8,128)}, u32[]{:S(2)}) copy-start(f32[1,8,256]{2,1,0:T(8,128)} %param.12) | copy-start | bytes 24580
  57.2 39.6 %copy-start.4 = (s32[1024]{0:T(1024)S(1)}, s32[1024]{0:T(1024)}, u32[]{:S(2)}) copy-start(s32[1024]{0:T(1024)} %param.17) | copy-start | bytes 12292
  57.2 35.2 %collective-permute-start.14 = (bf16[72,256]{1,0:T(8,128)(2,1)S(1)}, bf16[72,256]{1,0:T(8,128)(2,1)S(1)}, u32[]{:S(2)}, u32[]{:S(2)}) collective-permute-start(bf16[72,256]{1,0:T(8,128)(2,1)S(1)} %select_convert_fusion), channel_id=1, source_target_pairs={{0,4},{1,5},{2,6},{3,7},{8,12},{9,13},{10,14},{11,15},{16,20},{17,... | collective-permute-start | bytes 110600 | tf_op jit(solution)/shard_map/ppermute | solution.py:122
  93.4 7.5 %all-to-all-start.1 = ((f32[4,1,1024]{2,1,0:T(1,128)}), f32[4,1,1024]{2,1,0:T(1,128)S(1)}, u32[]{:S(2)}, u32[]{:S(2)}) async-start(f32[4,1,1024]{2,1,0:T(1,128)} %broadcast_in_dim.152), calls=%async_computation.1 | async-start | bytes 32768 | tf_op jit(solution)/shard_map/all_to_all | solution.py:159

commit v5 on v4

--- a/solution.py
+++ b/solution.py
@@ -8,7 +8,8 @@
 SUB = 8
 NZ, NY, NC, NX = 16, 4, 2, 4
 WIDTH = S // NX
-CARRY = WIDTH + SUB
+COLS = S // 2
+CARRY = COLS + SUB
 TM = ("z", "y", "core")
 FINE = lax.Precision.HIGH
 
@@ -35,13 +36,13 @@
     row = lax.broadcasted_iota(jnp.int32, (CARRY, S), 0)
     high = lax.reduce_precision(state, 8, 7)
     low = state - high
-    tail = jnp.where(row == WIDTH, high, jnp.where(row == WIDTH + 1, low, 0.0))
-    return jnp.where(row < WIDTH, cols, tail).astype(jnp.bfloat16)
+    tail = jnp.where(row == COLS, high, jnp.where(row == COLS + 1, low, 0.0))
+    return jnp.where(row < COLS, cols, tail).astype(jnp.bfloat16)
 
 
 def moved(outer, carry):
-    cols = jnp.dot(carry.astype(jnp.float32), outer[:S], precision=lax.Precision.HIGHEST)
-    state = cols[WIDTH : WIDTH + 1] + cols[WIDTH + 1 : WIDTH + 2] + outer[S : S + 1]
+    cols = jnp.dot(carry.astype(jnp.float32), outer[:S], precision=FINE)
+    state = cols[COLS : COLS + 1] + cols[COLS + 1 : COLS + 2] + outer[S : S + 1]
     return cols, state
 
 
@@ -76,7 +77,7 @@
     tail3 = after(pairs[1], tail2)
     plane = after(pairs[0], tail3)
 
-    top_cols = lax.dynamic_slice_in_dim(terminal_factor, x * WIDTH, WIDTH, 1).T
+    top_cols = lax.dynamic_slice_in_dim(terminal_factor, lax.rem(x, 2) * COLS, COLS, 1).T
     top = packed(
         jnp.concatenate([top_cols, jnp.zeros((SUB, S), jnp.float32)], axis=0), terminal_state[None, :]
     )
@@ -135,7 +136,7 @@
     )
     group = after(jnp.where(core == 0, mine, lone), beyond)
     cols, state = moved(group, entry)
-    factor_t = cols[:WIDTH].astype(jnp.bfloat16)
+    factor_t = cols[:COLS].astype(jnp.bfloat16)
     states = (state + sub_offset[0]).astype(jnp.bfloat16)
 
     rows_t = obs_rows.T
@@ -156,8 +157,7 @@
     projected = jnp.dot(factor_t, all_rows, preferred_element_type=jnp.float32)
     part = jnp.sum(projected * projected, axis=0)
     live = (jnp.arange(rows_t.shape[1]) < obs_count[0]).astype(jnp.float32)
-    parts = lax.all_to_all(jnp.broadcast_to(part, (NX, part.shape[0])), "col", 0, 0)
-    spread = (parts[0] + parts[1]) + (parts[2] + parts[3])
+    spread = part + lax.ppermute(part, "col", [(0, 1), (1, 0), (2, 3), (3, 2)])
     return (guess * live, spread * live)
 
 

time: 102 us -> 99.3 us (0.974)
  starting transfers between devices: 23 us -> 21.9 us
    all_to_all x1 -> x0, waiting for transfers between devices: 3.41 us -> none  [compute(): lax.all_to_all(jnp.broadcast_to(part, (NX, part.shape[0])), 'col', 0, 0)]
    all_to_all x1 -> x0, starting transfers between devices: 3.33 us -> none  [compute(): lax.all_to_all(jnp.broadcast_to(part, (NX, part.shape[0])), 'col', 0, 0)]
    ppermute x0 -> x1, starting transfers between devices: none -> 2.22 us  [compute(): spread = part + lax.ppermute(part, 'col', [(0, 1), (1, 0), (2, 3), (3, 2)])]
    ppermute x0 -> x1, waiting for transfers between devices: none -> 1.31 us  [compute(): spread = part + lax.ppermute(part, 'col', [(0, 1), (1, 0), (2, 3), (3, 2)])]
    ppermute x1, waiting for transfers between devices: 33.5 us -> 34.6 us  [compute(): crossed = lax.ppermute(entry, 'core', [(0, 1)])]
where the time goes in v5:
time: 99.3 us; the launch traced here: 98.9 us
  waiting for transfers between devices  41.3 us (42%)
  blocking collectives  24.3 us (24%)
  starting transfers between devices  21.9 us (22%)
  matrix products  5.46 us (5%)
  other arithmetic  3.31 us (3%)
  between operations  2.12 us (2%)
    ppermute x1, waiting for transfers between devices, compute(): crossed = lax.ppermute(entry, 'core', [(0, 1)])  34.6 us
    all_to_all x1, blocking collectives, compute(): lax.all_to_all(jnp.broadcast_to(own, (NY * NX, WIDTH + SUB, S)), ('y', 'c...  24.3 us
    ppermute x1, starting transfers between devices, compute(): other = lax.ppermute(own, 'core', [(0, 1), (1, 0)])  4.77 us
    ppermute x1, waiting for transfers between devices, compute(): swapped = lax.ppermute(rows_t, 'col', [(0, 1), (1, 0), (2, 3), (3, 2)])  3.88 us
    dot_general x12, matrix products, after(): return jnp.dot(inner, outer[:S], precision=FINE) + bias  3.52 us
    ppermute x1, starting transfers between devices, compute(): crossed_half = lax.ppermute(half, 'col', [(0, 2), (2, 0), (1, 3), (3, 1)])  2.76 us
    ppermute x1, starting transfers between devices, compute(): spread = part + lax.ppermute(part, 'col', [(0, 1), (1, 0), (2, 3), (3, 2)])  2.22 us
    ppermute x1, starting transfers between devices, compute(): swapped = lax.ppermute(rows_t, 'col', [(0, 1), (1, 0), (2, 3), (3, 2)])  2.12 us
  transfers between devices with their start and end apart: 18, of which 4 were waited for; matrix products, arithmetic and copies ran while one was open for 4% of the time, Pallas kernels for 0%

profile of v5, /device:TPU:1, one launch (start us, length us, event | category | flops | bytes accessed | tf_op | source)
XLA Modules:
  0.0 98.9 jit_solution(17145196266046990934)
XLA Ops:
  0.6 0.9 select_maximum_fusion
  1.7 24.3 %all_to_all.5 = f32[16,72,256]{2,1,0:T(8,128)S(1)} all-to-all(f32[16,72,256]{2,1,0:T(8,128)S(1)} %broadcast_in_dim.123), channel_id=1, replica_groups=mesh['z'=16,'y'=4,'core'=2,'col'=4] {'y','col'}, dimensions={0} | all-to-all | bytes 2359296 | tf_op jit(solution)/shard_map/all_to_all | solution.py:69
  26.0 4.8 %collective-permute-start = (f32[16,72,256]{2,1,0:T(8,128)S(1)}, f32[16,72,256]{2,1,0:T(8,128)S(1)}, u32[]{:S(2)}, u32[]{:S(2)}) collective-permute-start(f32[16,72,256]{2,1,0:T(8,128)S(1)} %all_to_all.5), channel_id=1, source_target_pairs={{0,4},{4,0},{1,5},{5,1},{2,6},{6,2},{3,7},{7,3},{8,12},{12,8},{9,1... | collective-permute-start | bytes 3538952 | tf_op jit(solution)/shard_map/ppermute | solution.py:72
  30.7 2.1 %collective-permute-start.15 = (bf16[64,1024]{1,0:T(8,128)(2,1)S(1)}, bf16[64,1024]{1,0:T(8,128)(2,1)S(1)}, u32[]{:S(2)}, u32[]{:S(2)}) collective-permute-start(bf16[64,1024]{1,0:T(8,128)(2,1)S(1)} %bitcast.80), channel_id=1, source_target_pairs={{0,1},{1,0},{2,3},{3,2},{4,5},{5,4},{6,7},{7,6},{8,9},{9,8},{10,11... | collective-permute-start | bytes 393224 | tf_op jit(solution)/shard_map/ppermute | solution.py:143
  33.8 3.9 %collective-permute-done.15 = bf16[64,1024]{1,0:T(8,128)(2,1)S(1)} collective-permute-done((bf16[64,1024]{1,0:T(8,128)(2,1)S(1)}, bf16[64,1024]{1,0:T(8,128)(2,1)S(1)}, u32[]{:S(2)}, u32[]{:S(2)}) %collective-permute-start.15) | collective-permute-done | bytes 131104 | tf_op jit(solution)/shard_map/ppermute | solution.py:143
  37.9 0.3 fusion.94
  38.2 0.3 convolution_add_fusion.10
  38.5 0.3 convolution_add_fusion.8
  38.8 0.3 convolution_add_fusion.11
  39.1 0.3 maximum_select_fusion
  39.4 0.3 convolution_add_fusion.9
  39.7 0.3 convolution_add_fusion.7
  40.0 0.3 convolution_add_fusion.5
  40.3 0.3 fusion.41
  40.7 0.7 collective-permute-start.1
  41.4 2.8 %collective-permute-start.16 = (bf16[128,1024]{1,0:T(8,128)(2,1)S(1)}, bf16[128,1024]{1,0:T(8,128)(2,1)S(1)}, u32[]{:S(2)}, u32[]{:S(2)}) collective-permute-start(bf16[128,1024]{1,0:T(8,128)(2,1)S(1)} %pad_maximum_fusion.3), channel_id=1, source_target_pairs={{0,2},{2,0},{1,3},{3,1},{4,6},{6,4},{5,7},{7,5},{8,10},{10,8},{9,1... | collective-permute-start | bytes 786440 | tf_op jit(solution)/shard_map/ppermute | solution.py:148
  44.2 0.7 collective-permute-start.6
  44.9 0.7 collective-permute-start.4
  45.6 0.2 fusion.39
  46.0 0.7 collective-permute-start.2
  46.7 0.3 convolution_add_fusion.3
  47.0 0.7 collective-permute-start.7
  47.7 0.3 convolution_add_fusion.4
  48.0 0.2 fusion.28
  48.3 0.7 collective-permute-start.5
  49.0 0.3 convolution_add_fusion.2
  49.3 0.2 fusion.35
  49.7 0.7 collective-permute-start.8
  50.4 1.4 %collective-permute-done.16 = bf16[128,1024]{1,0:T(8,128)(2,1)S(1)} collective-permute-done((bf16[128,1024]{1,0:T(8,128)(2,1)S(1)}, bf16[128,1024]{1,0:T(8,128)(2,1)S(1)}, u32[]{:S(2)}, u32[]{:S(2)}) %collective-permute-start.16) | collective-permute-done | bytes 262176 | tf_op jit(solution)/shard_map/ppermute | solution.py:148
  51.9 0.7 collective-permute-start.3
  52.6 0.7 collective-permute-start.13
  53.3 0.2 fusion.33
  53.7 0.7 collective-permute-start.10
  54.4 0.7 collective-permute-start.11
  55.1 0.7 collective-permute-start.12
  55.7 0.7 collective-permute-start.9
  56.4 0.3 fusion.1
  56.8 0.3 fusion.24
  57.2 1.3 %collective-permute-start.14 = (bf16[136,256]{1,0:T(8,128)(2,1)S(1)}, bf16[136,256]{1,0:T(8,128)(2,1)S(1)}, u32[]{:S(2)}, u32[]{:S(2)}) collective-permute-start(bf16[136,256]{1,0:T(8,128)(2,1)S(1)} %select_convert_fusion), channel_id=1, source_target_pairs={{0,4},{1,5},{2,6},{3,7},{8,12},{9,13},{10,14},{11,15},{16,20},{17,... | collective-permute-start | bytes 208904 | tf_op jit(solution)/shard_map/ppermute | solution.py:123
  58.5 0.3 convolution_add_fusion
  58.9 34.6 %collective-permute-done.14 = bf16[136,256]{1,0:T(8,128)(2,1)S(1)} collective-permute-done((bf16[136,256]{1,0:T(8,128)(2,1)S(1)}, bf16[136,256]{1,0:T(8,128)(2,1)S(1)}, u32[]{:S(2)}, u32[]{:S(2)}) %collective-permute-start.14) | collective-permute-done | bytes 69664 | tf_op jit(solution)/shard_map/ppermute | solution.py:123
  93.5 0.2 fusion.21
  93.7 0.2 fusion.2
  93.9 2.2 %collective-permute-start.17 = (f32[1024]{0:T(1024)S(1)}, f32[1024]{0:T(1024)S(1)}, u32[]{:S(2)}, u32[]{:S(2)}) collective-permute-start(f32[1024]{0:T(1024)S(1)} %fusion.2), channel_id=1, source_target_pairs={{0,1},{1,0},{2,3},{3,2},{4,5},{5,4},{6,7},{7,6},{8,9},{9,8},{10,11... | collective-permute-start | bytes 12296 | tf_op jit(solution)/shard_map/ppermute | solution.py:160
  96.2 0.2 fusion.3
  96.4 0.6 fusion.73
  97.0 1.3 %collective-permute-done.17 = f32[1024]{0:T(1024)S(1)} collective-permute-done((f32[1024]{0:T(1024)S(1)}, f32[1024]{0:T(1024)S(1)}, u32[]{:S(2)}, u32[]{:S(2)}) %collective-permute-start.17) | collective-permute-done | bytes 4128 | tf_op jit(solution)/shard_map/ppermute | solution.py:160
  98.3 0.6 add_select_fusion
  (62 shorter events, 1.5 us)
Async XLA Ops:
  0.6 32.3 %copy-start = (f32[256,256]{1,0:T(8,128)S(1)}, f32[256,256]{1,0:T(8,128)}, u32[]{:S(2)}) copy-start(f32[256,256]{1,0:T(8,128)} %param.14) | copy-start | bytes 786436
  1.6 29.1 %copy-start.1 = (bf16[1024,64]{0,1:T(8,128)(2,1)S(1)}, bf16[1024,64]{0,1:T(8,128)(2,1)}, u32[]{:S(2)}) copy-start(bf16[1024,64]{0,1:T(8,128)(2,1)} %param.15) | copy-start | bytes 393220
  1.6 31.3 %copy-start.2 = (f32[256]{0:T(256)S(1)}, f32[256]{0:T(256)}, u32[]{:S(2)}) copy-start(f32[256]{0:T(256)} %param.13) | copy-start | bytes 3076
  26.0 11.8 %collective-permute-start = (f32[16,72,256]{2,1,0:T(8,128)S(1)}, f32[16,72,256]{2,1,0:T(8,128)S(1)}, u32[]{:S(2)}, u32[]{:S(2)}) collective-permute-start(f32[16,72,256]{2,1,0:T(8,128)S(1)} %all_to_all.5), channel_id=1, source_target_pairs={{0,4},{4,0},{1,5},{5,1},{2,6},{6,2},{3,7},{7,3},{8,12},{12,8},{9,1... | collective-permute-start | bytes 3538952 | tf_op jit(solution)/shard_map/ppermute | solution.py:72
  30.7 6.9 %collective-permute-start.15 = (bf16[64,1024]{1,0:T(8,128)(2,1)S(1)}, bf16[64,1024]{1,0:T(8,128)(2,1)S(1)}, u32[]{:S(2)}, u32[]{:S(2)}) collective-permute-start(bf16[64,1024]{1,0:T(8,128)(2,1)S(1)} %bitcast.80), channel_id=1, source_target_pairs={{0,1},{1,0},{2,3},{3,2},{4,5},{5,4},{6,7},{7,6},{8,9},{9,8},{10,11... | collective-permute-start | bytes 393224 | tf_op jit(solution)/shard_map/ppermute | solution.py:143
  40.7 4.9 %collective-permute-start.1 = (bf16[136,256]{1,0:T(8,128)(2,1)S(1)}, bf16[136,256]{1,0:T(8,128)(2,1)S(1)}, u32[]{:S(2)}, u32[]{:S(2)}) collective-permute-start(bf16[136,256]{1,0:T(8,128)(2,1)S(1)} %select_convert_fusion.5), channel_id=1, source_target_pairs={{480,448},{488,456},{496,464},{504,472},{481,449},{489,457},{497,4... | collective-permute-start | bytes 208904 | tf_op jit(solution)/shard_map/ppermute | solution.py:91
  41.4 10.4 %collective-permute-start.16 = (bf16[128,1024]{1,0:T(8,128)(2,1)S(1)}, bf16[128,1024]{1,0:T(8,128)(2,1)S(1)}, u32[]{:S(2)}, u32[]{:S(2)}) collective-permute-start(bf16[128,1024]{1,0:T(8,128)(2,1)S(1)} %pad_maximum_fusion.3), channel_id=1, source_target_pairs={{0,2},{2,0},{1,3},{3,1},{4,6},{6,4},{5,7},{7,5},{8,10},{10,8},{9,1... | collective-permute-start | bytes 786440 | tf_op jit(solution)/shard_map/ppermute | solution.py:148
  44.2 2.4 %collective-permute-start.6 = (f32[264,256]{1,0:T(8,128)S(1)}, f32[264,256]{1,0:T(8,128)S(1)}, u32[]{:S(2)}, u32[]{:S(2)}) collective-permute-start(f32[264,256]{1,0:T(8,128)S(1)} %convolution_add_fusion.5), channel_id=1, source_target_pairs={{32,0},{40,8},{48,16},{56,24},{64,32},{72,40},{80,48},{88,56},{96,... | collective-permute-start | bytes 811016 | tf_op jit(solution)/shard_map/ppermute | solution.py:86
  44.9 2.8 %collective-permute-start.4 = (f32[264,256]{1,0:T(8,128)S(1)}, f32[264,256]{1,0:T(8,128)S(1)}, u32[]{:S(2)}, u32[]{:S(2)}) collective-permute-start(f32[264,256]{1,0:T(8,128)S(1)} %convolution_add_fusion.5), channel_id=1, source_target_pairs={{416,384},{424,392},{432,400},{440,408},{417,385},{425,393},{433,4... | collective-permute-start | bytes 811016 | tf_op jit(solution)/shard_map/ppermute | solution.py:89
  46.0 2.0 %collective-permute-start.2 = (bf16[136,256]{1,0:T(8,128)(2,1)S(1)}, bf16[136,256]{1,0:T(8,128)(2,1)S(1)}, u32[]{:S(2)}, u32[]{:S(2)}) collective-permute-start(bf16[136,256]{1,0:T(8,128)(2,1)S(1)} %select_convert_fusion.4), channel_id=1, source_target_pairs={{448,384},{456,392},{464,400},{472,408},{449,385},{457,393},{465,4... | collective-permute-start | bytes 208904 | tf_op jit(solution)/shard_map/ppermute | solution.py:93
  47.0 2.1 %collective-permute-start.7 = (f32[264,256]{1,0:T(8,128)S(1)}, f32[264,256]{1,0:T(8,128)S(1)}, u32[]{:S(2)}, u32[]{:S(2)}) collective-permute-start(f32[264,256]{1,0:T(8,128)S(1)} %convolution_add_fusion.3), channel_id=1, source_target_pairs={{64,0},{72,8},{80,16},{88,24},{192,128},{200,136},{208,144},{216,1... | collective-permute-start | bytes 811016 | tf_op jit(solution)/shard_map/ppermute | solution.py:99
  48.3 1.0 collective-permute-start.5
  49.7 3.6 %collective-permute-start.8 = (bf16[136,256]{1,0:T(8,128)(2,1)S(1)}, bf16[136,256]{1,0:T(8,128)(2,1)S(1)}, u32[]{:S(2)}, u32[]{:S(2)}) collective-permute-start(bf16[136,256]{1,0:T(8,128)(2,1)S(1)} %select_convert_fusion.2), channel_id=1, source_target_pairs={{256,128},{264,136},{272,144},{280,152},{257,129},{265,137},{273,1... | collective-permute-start | bytes 208904 | tf_op jit(solution)/shard_map/ppermute | solution.py:102
  51.9 4.8 %collective-permute-start.3 = (bf16[136,256]{1,0:T(8,128)(2,1)S(1)}, bf16[136,256]{1,0:T(8,128)(2,1)S(1)}, u32[]{:S(2)}, u32[]{:S(2)}) collective-permute-start(bf16[136,256]{1,0:T(8,128)(2,1)S(1)} %select_convert_fusion.4), channel_id=1, source_target_pairs={{448,416},{456,424},{464,432},{472,440},{449,417},{457,425},{465,4... | collective-permute-start | bytes 208904 | tf_op jit(solution)/shard_map/ppermute | solution.py:104
  52.6 3.1 %collective-permute-start.13 = (f32[264,256]{1,0:T(8,128)S(1)}, f32[264,256]{1,0:T(8,128)S(1)}, u32[]{:S(2)}, u32[]{:S(2)}) collective-permute-start(f32[264,256]{1,0:T(8,128)S(1)} %convolution_add_fusion.3), channel_id=1, source_target_pairs={{96,32},{104,40},{112,48},{120,56},{224,160},{232,168},{240,176},{... | collective-permute-start | bytes 811016 | tf_op jit(solution)/shard_map/ppermute | solution.py:103
  53.7 3.0 %collective-permute-start.10 = (bf16[136,256]{1,0:T(8,128)(2,1)S(1)}, bf16[136,256]{1,0:T(8,128)(2,1)S(1)}, u32[]{:S(2)}, u32[]{:S(2)}) collective-permute-start(bf16[136,256]{1,0:T(8,128)(2,1)S(1)} %fusion.49), channel_id=1, source_target_pairs={{128,64},{136,72},{144,80},{152,88},{256,192},{264,200},{272,208},... | collective-permute-start | bytes 208904 | tf_op jit(solution)/shard_map/ppermute | solution.py:116
  54.4 2.4 %collective-permute-start.11 = (bf16[136,256]{1,0:T(8,128)(2,1)S(1)}, bf16[136,256]{1,0:T(8,128)(2,1)S(1)}, u32[]{:S(2)}, u32[]{:S(2)}) collective-permute-start(bf16[136,256]{1,0:T(8,128)(2,1)S(1)} %fusion.49), channel_id=1, source_target_pairs={{128,32},{136,40},{144,48},{152,56},{256,160},{264,168},{272,176},... | collective-permute-start | bytes 208904 | tf_op jit(solution)/shard_map/ppermute | solution.py:116
  55.1 1.7 %collective-permute-start.12 = (bf16[136,256]{1,0:T(8,128)(2,1)S(1)}, bf16[136,256]{1,0:T(8,128)(2,1)S(1)}, u32[]{:S(2)}, u32[]{:S(2)}) collective-permute-start(bf16[136,256]{1,0:T(8,128)(2,1)S(1)} %fusion.49), channel_id=1, source_target_pairs={{128,0},{136,8},{144,16},{152,24},{129,1},{137,9},{145,17},{153,25... | collective-permute-start | bytes 208904 | tf_op jit(solution)/shard_map/ppermute | solution.py:113
  55.7 1.0 %collective-permute-start.9 = (bf16[136,256]{1,0:T(8,128)(2,1)S(1)}, bf16[136,256]{1,0:T(8,128)(2,1)S(1)}, u32[]{:S(2)}, u32[]{:S(2)}) collective-permute-start(bf16[136,256]{1,0:T(8,128)(2,1)S(1)} %fusion.49), channel_id=1, source_target_pairs={{128,96},{136,104},{144,112},{152,120},{256,224},{264,232},{272,24... | collective-permute-start | bytes 208904 | tf_op jit(solution)/shard_map/ppermute | solution.py:116
  57.2 36.2 %collective-permute-start.14 = (bf16[136,256]{1,0:T(8,128)(2,1)S(1)}, bf16[136,256]{1,0:T(8,128)(2,1)S(1)}, u32[]{:S(2)}, u32[]{:S(2)}) collective-permute-start(bf16[136,256]{1,0:T(8,128)(2,1)S(1)} %select_convert_fusion), channel_id=1, source_target_pairs={{0,4},{1,5},{2,6},{3,7},{8,12},{9,13},{10,14},{11,15},{16,20},{17,... | collective-permute-start | bytes 208904 | tf_op jit(solution)/shard_map/ppermute | solution.py:123
  58.8 37.3 %copy-start.3 = (f32[1,8,256]{2,1,0:T(8,128)S(1)}, f32[1,8,256]{2,1,0:T(8,128)}, u32[]{:S(2)}) copy-start(f32[1,8,256]{2,1,0:T(8,128)} %param.12) | copy-start | bytes 24580
  58.9 37.3 %copy-start.4 = (s32[1024]{0:T(1024)S(1)}, s32[1024]{0:T(1024)}, u32[]{:S(2)}) copy-start(s32[1024]{0:T(1024)} %param.17) | copy-start | bytes 12292
  93.9 4.4 %collective-permute-start.17 = (f32[1024]{0:T(1024)S(1)}, f32[1024]{0:T(1024)S(1)}, u32[]{:S(2)}, u32[]{:S(2)}) collective-permute-start(f32[1024]{0:T(1024)S(1)} %fusion.2), channel_id=1, source_target_pairs={{0,1},{1,0},{2,3},{3,2},{4,5},{5,4},{6,7},{7,6},{8,9},{9,8},{10,11... | collective-permute-start | bytes 12296 | tf_op jit(solution)/shard_map/ppermute | solution.py:160

commit v6 on v5

--- a/solution.py
+++ b/solution.py
@@ -23,7 +23,7 @@
 
 
 def tail_rows(vec):
-    return jnp.zeros((SUB, S), jnp.float32).at[0].set(vec)
+    return jnp.broadcast_to(vec[None, :], (SUB, S))
 
 
 def after(outer, inner):
@@ -50,9 +50,9 @@
     return packed(*moved(outer, carry))
 
 
-def maps_of(raw, y):
-    block = raw[y * NX : (y + 1) * NX, :WIDTH].reshape(S, S)
-    return jnp.concatenate([block, raw[y * NX, WIDTH:]], axis=0)
+def maps_of(raw):
+    raw = raw.reshape(NY, NX, WIDTH + SUB, S)
+    return raw[:, :, :WIDTH].reshape(NY, S, S), raw[:, 0, WIDTH:]
 
 
 def compute(
@@ -72,7 +72,10 @@
     other = lax.ppermute(own, "core", [(0, 1), (1, 0)])
     even = jnp.where(core == 0, own, other)
     odd = jnp.where(core == 0, other, own)
-    pairs = [after(maps_of(even, i), maps_of(odd, i)) for i in range(NY)]
+    (even_maps, even_tails), (odd_maps, odd_tails) = maps_of(even), maps_of(odd)
+    bodies = jnp.einsum("bij,bjk->bik", odd_maps, even_maps, precision=FINE)
+    tails = jnp.einsum("bij,bjk->bik", odd_tails, even_maps, precision=FINE) + even_tails
+    pairs = [jnp.concatenate([bodies[i], tails[i]], axis=0) for i in range(NY)]
     tail2 = after(pairs[2], pairs[3])
     tail3 = after(pairs[1], tail2)
     plane = after(pairs[0], tail3)

time: 99.3 us -> 107 us (1.078)
  waiting for transfers between devices: 41.3 us -> 48.3 us
    ppermute x1, waiting for transfers between devices: 1.45 us -> 6.77 us  [compute(): crossed_half = lax.ppermute(half, 'col', [(0, 2), (2, 0), (1, 3), (3, 1)])]
    dot_general x12 -> x8, matrix products: 3.52 us -> 2.34 us  [after(): return jnp.dot(inner, outer[:S], precision=FINE) + bias]
where the time goes in v6:
time: 107 us
  waiting for transfers between devices  48.3 us (45%)
  blocking collectives  24.3 us (23%)
  starting transfers between devices  22 us (21%)
  matrix products  5.28 us (5%)
  other arithmetic  3.33 us (3%)
  between operations  2.12 us (2%)
  local copies, waits for them, and re-layouts  1.3 us (1%)
    ppermute x1, waiting for transfers between devices, compute(): crossed = lax.ppermute(entry, 'core', [(0, 1)])  35.4 us
    all_to_all x1, blocking collectives, compute(): lax.all_to_all(jnp.broadcast_to(own, (NY * NX, WIDTH + SUB, S)), ('y', 'c...  24.3 us
    ppermute x1, waiting for transfers between devices, compute(): crossed_half = lax.ppermute(half, 'col', [(0, 2), (2, 0), (1, 3), (3, 1)])  6.77 us
    ppermute x1, starting transfers between devices, compute(): other = lax.ppermute(own, 'core', [(0, 1), (1, 0)])  4.9 us
    ppermute x1, waiting for transfers between devices, compute(): swapped = lax.ppermute(rows_t, 'col', [(0, 1), (1, 0), (2, 3), (3, 2)])  4.74 us
    ppermute x1, starting transfers between devices, compute(): crossed_half = lax.ppermute(half, 'col', [(0, 2), (2, 0), (1, 3), (3, 1)])  2.76 us
    dot_general x8, matrix products, after(): return jnp.dot(inner, outer[:S], precision=FINE) + bias  2.34 us
    ppermute x1, starting transfers between devices, compute(): spread = part + lax.ppermute(part, 'col', [(0, 1), (1, 0), (2, 3), (3, 2)])  2.19 us
  transfers between devices with their start and end apart: 18, of which 4 were waited for; matrix products, arithmetic and copies ran while one was open for 4% of the time, Pallas kernels for 0%

profile of v6, /device:TPU:1, one launch (start us, length us, event | category | flops | bytes accessed | tf_op | source)
XLA Modules:
  0.0 106.6 jit_solution(10031230772122532075)
XLA Ops:
  0.6 0.7 broadcast_in_dim.132
  1.4 0.8 pad_maximum_fusion.7
  2.3 24.3 %all_to_all.5 = f32[16,72,256]{2,1,0:T(8,128)S(1)} all-to-all(f32[16,72,256]{2,1,0:T(8,128)S(1)} %broadcast_in_dim.133), channel_id=1, replica_groups=mesh['z'=16,'y'=4,'core'=2,'col'=4] {'y','col'}, dimensions={0} | all-to-all | bytes 2359296 | tf_op jit(solution)/shard_map/all_to_all | solution.py:69
  26.6 4.9 %collective-permute-start = (f32[16,72,256]{2,1,0:T(8,128)S(1)}, f32[16,72,256]{2,1,0:T(8,128)S(1)}, u32[]{:S(2)}, u32[]{:S(2)}) collective-permute-start(f32[16,72,256]{2,1,0:T(8,128)S(1)} %all_to_all.5), channel_id=1, source_target_pairs={{0,4},{4,0},{1,5},{5,1},{2,6},{6,2},{3,7},{7,3},{8,12},{12,8},{9,1... | collective-permute-start | bytes 3538952 | tf_op jit(solution)/shard_map/ppermute | solution.py:72
  31.5 2.1 %collective-permute-start.15 = (bf16[64,1024]{1,0:T(8,128)(2,1)S(1)}, bf16[64,1024]{1,0:T(8,128)(2,1)S(1)}, u32[]{:S(2)}, u32[]{:S(2)}) collective-permute-start(bf16[64,1024]{1,0:T(8,128)(2,1)S(1)} %bitcast.88), channel_id=1, source_target_pairs={{0,1},{1,0},{2,3},{3,2},{4,5},{5,4},{6,7},{7,6},{8,9},{9,8},{10,11... | collective-permute-start | bytes 393224 | tf_op jit(solution)/shard_map/ppermute | solution.py:146
  33.7 4.7 %collective-permute-done.15 = bf16[64,1024]{1,0:T(8,128)(2,1)S(1)} collective-permute-done((bf16[64,1024]{1,0:T(8,128)(2,1)S(1)}, bf16[64,1024]{1,0:T(8,128)(2,1)S(1)}, u32[]{:S(2)}, u32[]{:S(2)}) %collective-permute-start.15) | collective-permute-done | bytes 131104 | tf_op jit(solution)/shard_map/ppermute | solution.py:146
  38.5 2.8 %collective-permute-start.16 = (bf16[128,1024]{1,0:T(8,128)(2,1)S(1)}, bf16[128,1024]{1,0:T(8,128)(2,1)S(1)}, u32[]{:S(2)}, u32[]{:S(2)}) collective-permute-start(bf16[128,1024]{1,0:T(8,128)(2,1)S(1)} %pad_maximum_fusion.4), channel_id=1, source_target_pairs={{0,2},{2,0},{1,3},{3,1},{4,6},{6,4},{5,7},{7,5},{8,10},{10,8},{9,1... | collective-permute-start | bytes 786440 | tf_op jit(solution)/shard_map/ppermute | solution.py:151
  42.1 6.8 %collective-permute-done.16 = bf16[128,1024]{1,0:T(8,128)(2,1)S(1)} collective-permute-done((bf16[128,1024]{1,0:T(8,128)(2,1)S(1)}, bf16[128,1024]{1,0:T(8,128)(2,1)S(1)}, u32[]{:S(2)}, u32[]{:S(2)}) %collective-permute-start.16) | collective-permute-done | bytes 262176 | tf_op jit(solution)/shard_map/ppermute | solution.py:151
  49.0 0.2 broadcast_select_fusion.1
  49.4 0.4 convolution_add_fusion.8
  49.8 0.6 fusion.79
  50.5 0.3 convolution_add_fusion.7
  50.8 0.3 convolution_add_fusion.6
  51.1 0.3 convolution_add_fusion.5
  51.4 0.7 collective-permute-start.6
  52.1 0.7 collective-permute-start.4
  52.8 0.3 fusion.27
  53.2 0.7 collective-permute-start.1
  53.9 0.2 fusion.25
  54.3 0.7 collective-permute-start.2
  55.0 0.3 convolution_add_fusion.3
  55.3 0.7 collective-permute-start.7
  56.0 0.3 convolution_add_fusion.4
  56.3 0.2 fusion.17
  56.7 0.7 collective-permute-start.5
  57.3 0.3 convolution_add_fusion.2
  57.6 0.2 fusion.21
  58.0 0.7 collective-permute-start.8
  58.8 0.7 collective-permute-start.3
  59.5 0.7 collective-permute-start.13
  60.2 0.2 fusion.19
  60.4 0.1 fusion.35
  60.5 0.7 collective-permute-start.10
  61.2 0.7 collective-permute-start.11
  61.9 0.7 collective-permute-start.12
  62.6 0.7 collective-permute-start.9
  63.3 0.3 fusion.1
  63.6 0.3 fusion.13
  64.1 1.3 %collective-permute-start.14 = (bf16[136,256]{1,0:T(8,128)(2,1)S(1)}, bf16[136,256]{1,0:T(8,128)(2,1)S(1)}, u32[]{:S(2)}, u32[]{:S(2)}) collective-permute-start(bf16[136,256]{1,0:T(8,128)(2,1)S(1)} %select_convert_fusion), channel_id=1, source_target_pairs={{0,4},{1,5},{2,6},{3,7},{8,12},{9,13},{10,14},{11,15},{16,20},{17,... | collective-permute-start | bytes 208904 | tf_op jit(solution)/shard_map/ppermute | solution.py:126
  65.4 0.3 convolution_add_fusion
  65.8 35.4 %collective-permute-done.14 = bf16[136,256]{1,0:T(8,128)(2,1)S(1)} collective-permute-done((bf16[136,256]{1,0:T(8,128)(2,1)S(1)}, bf16[136,256]{1,0:T(8,128)(2,1)S(1)}, u32[]{:S(2)}, u32[]{:S(2)}) %collective-permute-start.14) | collective-permute-done | bytes 69664 | tf_op jit(solution)/shard_map/ppermute | solution.py:126
  101.1 0.2 fusion.10
  101.4 0.2 fusion.2
  101.6 2.2 %collective-permute-start.17 = (f32[1024]{0:T(1024)S(1)}, f32[1024]{0:T(1024)S(1)}, u32[]{:S(2)}, u32[]{:S(2)}) collective-permute-start(f32[1024]{0:T(1024)S(1)} %fusion.2), channel_id=1, source_target_pairs={{0,1},{1,0},{2,3},{3,2},{4,5},{5,4},{6,7},{7,6},{8,9},{9,8},{10,11... | collective-permute-start | bytes 12296 | tf_op jit(solution)/shard_map/ppermute | solution.py:163
  103.8 0.2 fusion.3
  104.0 0.6 fusion.59
  104.6 1.3 %collective-permute-done.17 = f32[1024]{0:T(1024)S(1)} collective-permute-done((f32[1024]{0:T(1024)S(1)}, f32[1024]{0:T(1024)S(1)}, u32[]{:S(2)}, u32[]{:S(2)}) %collective-permute-start.17) | collective-permute-done | bytes 4128 | tf_op jit(solution)/shard_map/ppermute | solution.py:163
  106.0 0.6 add_select_fusion
  (67 shorter events, 1.6 us)
Async XLA Ops:
  0.6 33.1 %copy-start = (f32[256,256]{1,0:T(8,128)S(1)}, f32[256,256]{1,0:T(8,128)}, u32[]{:S(2)}) copy-start(f32[256,256]{1,0:T(8,128)} %param.12) | copy-start | bytes 786436
  2.3 29.2 %copy-start.3 = (bf16[1024,64]{0,1:T(8,128)(2,1)S(1)}, bf16[1024,64]{0,1:T(8,128)(2,1)}, u32[]{:S(2)}) copy-start(bf16[1024,64]{0,1:T(8,128)(2,1)} %param.13) | copy-start | bytes 393220
  26.6 15.5 %copy-start.4 = (f32[256]{0:T(256)S(1)}, f32[256]{0:T(256)}, u32[]{:S(2)}) copy-start(f32[256]{0:T(256)} %param.11) | copy-start | bytes 3076
  26.6 22.4 %collective-permute-start = (f32[16,72,256]{2,1,0:T(8,128)S(1)}, f32[16,72,256]{2,1,0:T(8,128)S(1)}, u32[]{:S(2)}, u32[]{:S(2)}) collective-permute-start(f32[16,72,256]{2,1,0:T(8,128)S(1)} %all_to_all.5), channel_id=1, source_target_pairs={{0,4},{4,0},{1,5},{5,1},{2,6},{6,2},{3,7},{7,3},{8,12},{12,8},{9,1... | collective-permute-start | bytes 3538952 | tf_op jit(solution)/shard_map/ppermute | solution.py:72
  31.5 6.9 %collective-permute-start.15 = (bf16[64,1024]{1,0:T(8,128)(2,1)S(1)}, bf16[64,1024]{1,0:T(8,128)(2,1)S(1)}, u32[]{:S(2)}, u32[]{:S(2)}) collective-permute-start(bf16[64,1024]{1,0:T(8,128)(2,1)S(1)} %bitcast.88), channel_id=1, source_target_pairs={{0,1},{1,0},{2,3},{3,2},{4,5},{5,4},{6,7},{7,6},{8,9},{9,8},{10,11... | collective-permute-start | bytes 393224 | tf_op jit(solution)/shard_map/ppermute | solution.py:146
  38.5 10.4 %collective-permute-start.16 = (bf16[128,1024]{1,0:T(8,128)(2,1)S(1)}, bf16[128,1024]{1,0:T(8,128)(2,1)S(1)}, u32[]{:S(2)}, u32[]{:S(2)}) collective-permute-start(bf16[128,1024]{1,0:T(8,128)(2,1)S(1)} %pad_maximum_fusion.4), channel_id=1, source_target_pairs={{0,2},{2,0},{1,3},{3,1},{4,6},{6,4},{5,7},{7,5},{8,10},{10,8},{9,1... | collective-permute-start | bytes 786440 | tf_op jit(solution)/shard_map/ppermute | solution.py:151
  51.4 3.5 %collective-permute-start.6 = (f32[264,256]{1,0:T(8,128)S(1)}, f32[264,256]{1,0:T(8,128)S(1)}, u32[]{:S(2)}, u32[]{:S(2)}) collective-permute-start(f32[264,256]{1,0:T(8,128)S(1)} %convolution_add_fusion.5), channel_id=1, source_target_pairs={{32,0},{40,8},{48,16},{56,24},{64,32},{72,40},{80,48},{88,56},{96,... | collective-permute-start | bytes 811016 | tf_op jit(solution)/shard_map/ppermute | solution.py:89
  52.1 3.9 %collective-permute-start.4 = (f32[264,256]{1,0:T(8,128)S(1)}, f32[264,256]{1,0:T(8,128)S(1)}, u32[]{:S(2)}, u32[]{:S(2)}) collective-permute-start(f32[264,256]{1,0:T(8,128)S(1)} %convolution_add_fusion.5), channel_id=1, source_target_pairs={{416,384},{424,392},{432,400},{440,408},{417,385},{425,393},{433,4... | collective-permute-start | bytes 811016 | tf_op jit(solution)/shard_map/ppermute | solution.py:92
  53.2 0.7 collective-permute-start.1
  54.3 2.0 %collective-permute-start.2 = (bf16[136,256]{1,0:T(8,128)(2,1)S(1)}, bf16[136,256]{1,0:T(8,128)(2,1)S(1)}, u32[]{:S(2)}, u32[]{:S(2)}) collective-permute-start(bf16[136,256]{1,0:T(8,128)(2,1)S(1)} %select_convert_fusion.4), channel_id=1, source_target_pairs={{448,384},{456,392},{464,400},{472,408},{449,385},{457,393},{465,4... | collective-permute-start | bytes 208904 | tf_op jit(solution)/shard_map/ppermute | solution.py:96
  55.3 2.0 %collective-permute-start.7 = (f32[264,256]{1,0:T(8,128)S(1)}, f32[264,256]{1,0:T(8,128)S(1)}, u32[]{:S(2)}, u32[]{:S(2)}) collective-permute-start(f32[264,256]{1,0:T(8,128)S(1)} %convolution_add_fusion.3), channel_id=1, source_target_pairs={{64,0},{72,8},{80,16},{88,24},{192,128},{200,136},{208,144},{216,1... | collective-permute-start | bytes 811016 | tf_op jit(solution)/shard_map/ppermute | solution.py:102
  56.7 1.0 collective-permute-start.5
  58.0 2.2 %collective-permute-start.8 = (bf16[136,256]{1,0:T(8,128)(2,1)S(1)}, bf16[136,256]{1,0:T(8,128)(2,1)S(1)}, u32[]{:S(2)}, u32[]{:S(2)}) collective-permute-start(bf16[136,256]{1,0:T(8,128)(2,1)S(1)} %select_convert_fusion.2), channel_id=1, source_target_pairs={{256,128},{264,136},{272,144},{280,152},{257,129},{265,137},{273,1... | collective-permute-start | bytes 208904 | tf_op jit(solution)/shard_map/ppermute | solution.py:105
  58.8 4.8 %copy-start.1 = (f32[264,256]{1,0:T(8,128)}, f32[264,256]{1,0:T(8,128)S(1)}, u32[]{:S(2)}) copy-start(f32[264,256]{1,0:T(8,128)S(1)} %fusion.9) | copy-start | bytes 811012
  58.8 4.8 %collective-permute-start.3 = (bf16[136,256]{1,0:T(8,128)(2,1)S(1)}, bf16[136,256]{1,0:T(8,128)(2,1)S(1)}, u32[]{:S(2)}, u32[]{:S(2)}) collective-permute-start(bf16[136,256]{1,0:T(8,128)(2,1)S(1)} %select_convert_fusion.4), channel_id=1, source_target_pairs={{448,416},{456,424},{464,432},{472,440},{449,417},{457,425},{465,4... | collective-permute-start | bytes 208904 | tf_op jit(solution)/shard_map/ppermute | solution.py:107
  59.5 3.1 %collective-permute-start.13 = (f32[264,256]{1,0:T(8,128)S(1)}, f32[264,256]{1,0:T(8,128)S(1)}, u32[]{:S(2)}, u32[]{:S(2)}) collective-permute-start(f32[264,256]{1,0:T(8,128)S(1)} %convolution_add_fusion.3), channel_id=1, source_target_pairs={{96,32},{104,40},{112,48},{120,56},{224,160},{232,168},{240,176},{... | collective-permute-start | bytes 811016 | tf_op jit(solution)/shard_map/ppermute | solution.py:106
  60.5 3.1 %collective-permute-start.10 = (bf16[136,256]{1,0:T(8,128)(2,1)S(1)}, bf16[136,256]{1,0:T(8,128)(2,1)S(1)}, u32[]{:S(2)}, u32[]{:S(2)}) collective-permute-start(bf16[136,256]{1,0:T(8,128)(2,1)S(1)} %fusion.35), channel_id=1, source_target_pairs={{128,64},{136,72},{144,80},{152,88},{256,192},{264,200},{272,208},... | collective-permute-start | bytes 208904 | tf_op jit(solution)/shard_map/ppermute | solution.py:119
  61.2 2.4 %collective-permute-start.11 = (bf16[136,256]{1,0:T(8,128)(2,1)S(1)}, bf16[136,256]{1,0:T(8,128)(2,1)S(1)}, u32[]{:S(2)}, u32[]{:S(2)}) collective-permute-start(bf16[136,256]{1,0:T(8,128)(2,1)S(1)} %fusion.35), channel_id=1, source_target_pairs={{128,32},{136,40},{144,48},{152,56},{256,160},{264,168},{272,176},... | collective-permute-start | bytes 208904 | tf_op jit(solution)/shard_map/ppermute | solution.py:119
  61.9 1.7 %collective-permute-start.12 = (bf16[136,256]{1,0:T(8,128)(2,1)S(1)}, bf16[136,256]{1,0:T(8,128)(2,1)S(1)}, u32[]{:S(2)}, u32[]{:S(2)}) collective-permute-start(bf16[136,256]{1,0:T(8,128)(2,1)S(1)} %fusion.35), channel_id=1, source_target_pairs={{128,0},{136,8},{144,16},{152,24},{129,1},{137,9},{145,17},{153,25... | collective-permute-start | bytes 208904 | tf_op jit(solution)/shard_map/ppermute | solution.py:116
  62.6 1.1 collective-permute-start.9
  63.6 1.8 %copy-start.2 = (f32[264,256]{1,0:T(8,128)S(1)}, f32[264,256]{1,0:T(8,128)}, u32[]{:S(2)}) copy-start(f32[264,256]{1,0:T(8,128)} %copy-done.1) | copy-start | bytes 811012
  63.6 1.8 %slice-start = ((f32[264,256]{1,0:T(8,128)}), f32[8,256]{1,0:T(8,128)S(1)}, s32[]{:S(2)}) async-start(f32[264,256]{1,0:T(8,128)} %copy-done.1), calls=%async_computation.1 | async-start | bytes 16384 | tf_op jit(solution)/shard_map/slice | solution.py:31
  64.1 37.1 %collective-permute-start.14 = (bf16[136,256]{1,0:T(8,128)(2,1)S(1)}, bf16[136,256]{1,0:T(8,128)(2,1)S(1)}, u32[]{:S(2)}, u32[]{:S(2)}) collective-permute-start(bf16[136,256]{1,0:T(8,128)(2,1)S(1)} %select_convert_fusion), channel_id=1, source_target_pairs={{0,4},{1,5},{2,6},{3,7},{8,12},{9,13},{10,14},{11,15},{16,20},{17,... | collective-permute-start | bytes 208904 | tf_op jit(solution)/shard_map/ppermute | solution.py:126
  65.7 38.1 %copy-start.5 = (f32[1,8,256]{2,1,0:T(8,128)S(1)}, f32[1,8,256]{2,1,0:T(8,128)}, u32[]{:S(2)}) copy-start(f32[1,8,256]{2,1,0:T(8,128)} %param.10) | copy-start | bytes 24580
  65.7 38.1 %copy-start.6 = (s32[1024]{0:T(1024)S(1)}, s32[1024]{0:T(1024)}, u32[]{:S(2)}) copy-start(s32[1024]{0:T(1024)} %param.15) | copy-start | bytes 12292
  101.6 4.4 %collective-permute-start.17 = (f32[1024]{0:T(1024)S(1)}, f32[1024]{0:T(1024)S(1)}, u32[]{:S(2)}, u32[]{:S(2)}) collective-permute-start(f32[1024]{0:T(1024)S(1)} %fusion.2), channel_id=1, source_target_pairs={{0,1},{1,0},{2,3},{3,2},{4,5},{5,4},{6,7},{7,6},{8,9},{9,8},{10,11... | collective-permute-start | bytes 12296 | tf_op jit(solution)/shard_map/ppermute | solution.py:163
